TPU v7x, 32 devices: a whole 2x2x4 slice. The times are simulated.
32 devices in a mesh: tm: 16 (over z, x, core), chan: 2 (over y).
Axes of the slice: x: 2, y: 2, z: 4, core: 2. Of those that a mesh axis runs over, the one named last changes fastest.
Arguments:
- series: float32 [64, 8192], P('chan', 'tm'), may hold values from -200 to 200
- tail: float32 [64, 127], P('chan'), may hold values from -200 to 200
- excl: int32 [1], replicated, may hold values from 32 to 128
Outputs:
- profile: float32 [8192], P('tm')
All inputs are finite; a program needn't handle non-finite values.
Results may differ from a plain program's by a relative error of at most 0.0003.
Values may be sent and summed in bfloat16 or wider, within the bound.
No kernel may reach another device: no remote copies, remote signals or barrier semaphores. Data moves between devices by JAX's collectives and lax.ppermute only.
A program may use at most 128 MiB of HBM per device.

v0:
```python
import math

import jax
import jax.numpy as jnp
from jax import lax
from jax.sharding import PartitionSpec as P

C = 64


EPSILON = 1e-05
CEILING = 4.0


def from_behind(shard, axis, by):
    length = lax.axis_size(axis)
    pairs = [(i, i + by) for i in range(length) if 0 <= i + by < length]
    return lax.ppermute(shard, axis, pairs)


def normalize(extended, count, length, channels):
    starts = (
        jnp.arange(length, dtype=jnp.int32)[:, None] + jnp.arange(count, dtype=jnp.int32)[None, :]
    )
    windows = extended[:, starts]
    center = jnp.mean(windows, axis=1, keepdims=True)
    shifted = windows - center
    spread = jnp.mean(shifted * shifted, axis=1, keepdims=True)
    factor = lax.rsqrt(spread + EPSILON) * (1.0 / math.sqrt(length * channels))
    return (shifted * factor).astype(jnp.bfloat16)


def correlate(left, right):
    return lax.dot_general(
        left, right, (((0, 1), (0, 1)), ((), ())), preferred_element_type=jnp.float32
    )


def on_device(series, tail, excl):
    count = series.shape[1]
    width = tail.shape[1]
    length = width + 1
    blocks = lax.axis_size("tm")
    block_index = lax.axis_index("tm")
    head = from_behind(series[:, :width], "tm", -1)
    head = jnp.where(block_index == blocks - 1, tail, head)
    extended = jnp.concatenate([series, head], axis=1)
    query = normalize(extended, count, length, C)
    nearby = from_behind(query, "tm", -1)
    faraway = from_behind(query, "tm", -2)
    limit = excl[0]

    def scored(total, row_pos, offset):
        columns = (block_index + offset) * count + jnp.arange(count, dtype=jnp.int32)[None, :]
        keep = (jnp.abs(row_pos - columns) >= limit) & (block_index + offset < blocks)
        return jnp.where(keep, 1.0 - total, CEILING)

    row_pos = block_index * count + jnp.arange(count, dtype=jnp.int32)[:, None]

    def summed(right, offset):
        total = lax.psum(correlate(query, right), "chan")
        return scored(total, row_pos, offset)

    own_scores = summed(query, 0)
    near_scores = summed(nearby, 1)
    far_scores = summed(faraway, 2)
    row_best = jnp.minimum(
        jnp.min(own_scores, axis=1),
        jnp.minimum(jnp.min(near_scores, axis=1), jnp.min(far_scores, axis=1)),
    )
    near_cols = jnp.min(near_scores, axis=0)
    far_cols = jnp.min(far_scores, axis=0)
    near_home = from_behind(CEILING - near_cols, "tm", 1)
    far_home = from_behind(CEILING - far_cols, "tm", 2)
    return jnp.minimum(row_best, jnp.minimum(CEILING - near_home, CEILING - far_home))


def solution(mesh):
    placed = (P("chan", "tm"), P("chan", None), P())
    return jax.shard_map(on_device, mesh=mesh, in_specs=placed, out_specs=P("tm"), check_vma=False)
```

profile of v0, /device:TPU:0, one launch (start us, length us, event | category | flops | bytes accessed | tf_op | source)
XLA Modules:
  0.0 509.8 jit_solution(10372994987045576951)
XLA Ops:
  6.5 0.7 slice.3
  7.3 1.3 collective-permute-start
  8.7 1.6 collective-permute-done
  10.3 0.8 pad_maximum_fusion
  11.2 0.2 copy.18
  11.3 215.5 %gather_fusion = f32[65536,32]{1,0:T(8,128)} fusion(f32[32,639]{0,1:T(8,128)S(1)} %copy.18, s32[65536]{0:T(1024)S(1)} %broadcast_clamp_fusion), kind=kCustom, calls=%fused_computation | custom fusion | bytes 17039360 | tf_op jit(solution)/shard_map/gather | solution.py:25
  226.8 22.1 %copy.26 = f32[128,512,32]{1,0,2:T(8,128)} copy(f32[128,512,32]{2,1,0:T(8,128)} %bitcast.26) | data formatting | bytes 16777216 | tf_op jit(solution)/shard_map/gather | solution.py:25
  249.0 4.7 bitcast_reduce_fusion
  253.7 1.0 copy-done
  254.7 1.4 multiply_reduce_fusion
  256.2 1.7 multiply_convert_fusion
  257.9 1.3 collective-permute-start.1
  259.2 1.5 collective-permute-start.2
  260.7 3.4 convolution_bitcast_fusion.2
  264.1 5.7 %collective-permute-done.1 = bf16[32,128,512]{2,1,0:T(8,128)(2,1)S(1)} collective-permute-done((bf16[32,128,512]{2,1,0:T(8,128)(2,1)S(1)}, bf16[32,128,512]{2,1,0:T(8,128)(2,1)S(1)}, u32[]{:S(2)}, u32[]{:S(2)}) %collective-permute-start.1) | collective-permute-done | bytes 4194336 | tf_op jit(solution)/shard_map/ppermute | solution.py:18
  269.8 3.3 convolution_bitcast_fusion.1
  273.1 128.0 %collective-permute-done.2 = bf16[32,128,512]{2,1,0:T(8,128)(2,1)S(1)} collective-permute-done((bf16[32,128,512]{2,1,0:T(8,128)(2,1)S(1)}, bf16[32,128,512]{2,1,0:T(8,128)(2,1)S(1)}, u32[]{:S(2)}, u32[]{:S(2)}) %collective-permute-start.2) | collective-permute-done | bytes 4194336 | tf_op jit(solution)/shard_map/ppermute | solution.py:18
  401.1 3.4 convolution_bitcast_fusion
  405.2 87.3 %all-reduce.3.cloned.1.call-done = (f32[512,512]{1,0:T(8,128)}, f32[512,512]{1,0:T(8,128)}, f32[512,512]{1,0:T(8,128)}) async-done(((f32[512,512]{1,0:T(8,128)}, f32[512,512]{1,0:T(8,128)}, f32[512,512]{1,0:T(8,128)}), (f32[512,512]{1,0:T(8,128)}, f32[512,512]{1,0:T(8,128)}, f32[512,512]{1,0:T(8,128)})) %all-reduce.3.cloned.1.call-update) | async-done | bytes 3145744 | tf_op jit(solution)/shard_map/psum | solution.py:61
  492.5 3.2 fusion.6
  495.7 1.6 collective-permute-start.3
  497.3 3.7 collective-permute-start.4
  501.0 1.3 collective-permute-done.4
  502.3 0.6 minimum_minimum_fusion
  (14 shorter events, 0.2 us)
Async XLA Ops:
  6.5 486.0 %all-reduce.3.cloned.1.call-start = ((), (), s32[]{:S(2)}) async-start(), calls=%async_computation | async-start | bytes 6291456 | tf_op jit(solution)/shard_map/psum | solution.py:61
  7.3 3.1 collective-permute-start
  249.0 5.8 %copy-start = (f32[128,512,32]{1,0,2:T(8,128)S(1)}, f32[128,512,32]{1,0,2:T(8,128)}, u32[]{:S(2)}) copy-start(f32[128,512,32]{1,0,2:T(8,128)} %copy.26) | copy-start | bytes 25165828
  257.9 11.9 %collective-permute-start.1 = (bf16[32,128,512]{2,1,0:T(8,128)(2,1)S(1)}, bf16[32,128,512]{2,1,0:T(8,128)(2,1)S(1)}, u32[]{:S(2)}, u32[]{:S(2)}) collective-permute-start(bf16[32,128,512]{2,1,0:T(8,128)(2,1)S(1)} %multiply_convert_fusion), channel_id=1, source_target_pairs={{2,0},{4,2},{6,4},{8,6},{10,8},{12,10},{14,12},{16,14},{18,16},{20... | collective-permute-start | bytes 12582920 | tf_op jit(solution)/shard_map/ppermute | solution.py:18
  259.2 141.9 %collective-permute-start.2 = (bf16[32,128,512]{2,1,0:T(8,128)(2,1)S(1)}, bf16[32,128,512]{2,1,0:T(8,128)(2,1)S(1)}, u32[]{:S(2)}, u32[]{:S(2)}) collective-permute-start(bf16[32,128,512]{2,1,0:T(8,128)(2,1)S(1)} %multiply_convert_fusion), channel_id=1, source_target_pairs={{4,0},{6,2},{8,4},{10,6},{12,8},{14,10},{16,12},{18,14},{20,16},{2... | collective-permute-start | bytes 12582920 | tf_op jit(solution)/shard_map/ppermute | solution.py:18
  495.7 5.3 %collective-permute-start.3 = (f32[512]{0:T(512)S(1)}, f32[512]{0:T(512)S(1)}, u32[]{:S(2)}, u32[]{:S(2)}) collective-permute-start(f32[512]{0:T(512)S(1)} %broadcast_subtract_fusion.1), channel_id=1, source_target_pairs={{0,2},{2,4},{4,6},{6,8},{8,10},{10,12},{12,14},{14,16},{16,18},{18... | collective-permute-start | bytes 6152 | tf_op jit(solution)/shard_map/ppermute | solution.py:18
  497.3 5.0 collective-permute-start.4
Sparse Core Ops, SparseCore 0:
  404.6 87.8 all-reduce.2
where the time goes:
time: 511 us; the launch traced here: 510 us
  local copies, waits for them, and re-layouts  240 us (47%)
  waiting for transfers between devices  224 us (44%)
  between operations  14.2 us (3%)
  other arithmetic  12.6 us (2%)
  matrix products  10.1 us (2%)
  starting transfers between devices  9.34 us (2%)
    gather x2, local copies, waits for them, and re-layouts, normalize(): windows = extended[:, starts]  238 us
    ppermute x5, waiting for transfers between devices, from_behind(): return lax.ppermute(shard, axis, pairs)  137 us
    psum x1, waiting for transfers between devices, summed(): total = lax.psum(correlate(query, right), 'chan')  87.3 us
  transfers between devices with their start and end apart: 6, of which 5 were waited for; matrix products, arithmetic and copies ran while one was open for 1% of the time, Pallas kernels for 0%

commit v1 on v0

v1 whole, which is shorter than its diff:
```python
import functools
import math

import jax
import jax.numpy as jnp
from jax import lax
from jax.experimental import pallas as pl
from jax.experimental.pallas import tpu as pltpu
from jax.sharding import PartitionSpec as P

EPSILON = 1e-05
CEILING = 4.0
LANES = 128
STEPS = 8


def transposed(source, target):
    channels, length = source.shape
    half = LANES // 2
    value = source[...]
    ahead = pltpu.roll(value, length - half, 1)
    for start in range(0, length, LANES):
        stop = start + LANES
        both = jnp.concatenate([value[:, start:stop], ahead[:, start:stop]], axis=0)
        target[start:stop, :] = both.T


def statistics(samples, sums, moments, mean, scale, count, window, channels):
    half = window // 2
    current = samples
    size = 1
    level = 0
    while size < half:
        rows = -(-(count + half - 2 * size) // 8) * 8
        for start in range(0, rows, 64):
            stop = min(start + 64, rows)
            here = current[start:stop, :]
            there = current[start + size : stop + size, :]
            gap = here - there
            square = gap * gap
            if size > 1:
                old = moments[level % 2]
                square += 2.0 * (old[start:stop, :] + old[start + size : stop + size, :])
            sums[(level + 1) % 2][start:stop, :] = here + there
            moments[(level + 1) % 2][start:stop, :] = square
        level += 1
        current = sums[level % 2]
        size *= 2
    for start in range(0, count, 64):
        here = current[start : start + 64, :]
        there = pltpu.roll(here, LANES // 2, 1)
        gap = here - there
        old = moments[level % 2][start : start + 64, :]
        total = gap * gap + 2.0 * (old + pltpu.roll(old, LANES // 2, 1))
        mean[start : start + 64, :] = (here + there) * (1.0 / window)
        spread = total * (1.0 / (window * window))
        scale[start : start + 64, :] = lax.rsqrt(spread + EPSILON) * (
            1.0 / math.sqrt(window * channels)
        )


def contract(left, right):
    return lax.dot_general(
        left, right, (((1,), (1,)), ((), ())), preferred_element_type=jnp.float32
    )


def body(
    info, near, other, own_out, other_out, samples, means, scales,
    sums_a, sums_b, moments_a, moments_b, zed_a, zed_b, cross, strip, patch,
):
    channels = near.shape[0]
    count = means.shape[1]
    window = 2 * (near.shape[1] - count) // 2
    limit, chan, shift, valid = info[0], info[1], info[2], info[3]
    for index, source in enumerate((near, other)):
        transposed(source, samples.at[index])
        statistics(
            samples.at[index], (sums_a, sums_b), (moments_a, moments_b),
            means.at[index], scales.at[index], count, window, channels,
        )

    def fill(step, zed):
        for index in range(2):
            for start in range(0, count, 16):
                mean = means[index, start : start + 16, :]
                scale = scales[index, start : start + 16, :]
                for inner in range(STEPS):
                    x = samples[index, pl.ds(step * STEPS + (start + inner), 16), :]
                    row = index * count + start
                    zed[row : row + 16, inner * LANES : (inner + 1) * LANES] = (
                        (x - mean) * scale
                    ).astype(jnp.bfloat16)

    def multiply(zed):
        mine = zed[:count, :]
        quarter = count // 4
        cross[...] += contract(zed[count:, :], mine)
        first = pl.multiple_of(chan * quarter, quarter)
        strip[...] += contract(zed[pl.ds(first, quarter), :], mine)
        second = pl.multiple_of(2 * quarter + chan * quarter, quarter)
        patch[...] += contract(zed[pl.ds(second, quarter), :], zed[2 * quarter : count, :])

    cross[...] = jnp.zeros_like(cross)
    strip[...] = jnp.zeros_like(strip)
    patch[...] = jnp.zeros_like(patch)
    fill(0, zed_a)
    rounds = window // 2 // STEPS // 2

    def loop(index, carry):
        fill(2 * index + 1, zed_b)
        multiply(zed_a)
        fill(2 * index + 2, zed_a)
        multiply(zed_b)
        return carry

    lax.fori_loop(0, rounds, loop, 0)

    floor = 1.0 - CEILING
    quarter = count // 4

    def gap(shape, row_start, column_start):
        rows = lax.broadcasted_iota(jnp.int32, shape, 0) + row_start
        columns = lax.broadcasted_iota(jnp.int32, shape, 1) + column_start
        return rows - columns

    def lanes(value):
        best = value[:, :LANES]
        for start in range(LANES, value.shape[1], LANES):
            best = jnp.maximum(best, value[:, start : start + LANES])
        return jnp.max(best.T, axis=0, keepdims=True)

    far = jnp.where(
        (gap(cross.shape, shift * count, 0) >= limit) & (valid > 0), cross[...], floor
    )
    columns = jnp.max(far, axis=0, keepdims=True)
    for index in range(4):
        part = far[index * quarter : (index + 1) * quarter, :]
        other_out[index : index + 1, :] = 1.0 - lanes(part)
    first = jnp.where(jnp.abs(gap(strip.shape, chan * quarter, 0)) >= limit, strip[...], floor)
    columns = jnp.maximum(columns, jnp.max(first, axis=0, keepdims=True))
    second = jnp.where(jnp.abs(gap(patch.shape, chan * quarter, 0)) >= limit, patch[...], floor)
    last = jnp.maximum(columns[:, 2 * quarter :], jnp.max(second, axis=0, keepdims=True))
    pieces = [
        columns[:, :quarter], columns[:, quarter : 2 * quarter],
        last[:, :quarter], last[:, quarter:],
    ]
    lines = [lanes(first), lanes(second)]
    for index in range(4):
        line = jnp.where(chan == index % 2, lines[index // 2], floor)
        own_out[index : index + 1, :] = 1.0 - jnp.maximum(pieces[index], line)


def scores(info, near, other, count):
    channels, length = near.shape
    window = length - count
    wide = STEPS * LANES
    quarter = count // 4
    vmem = pl.BlockSpec(memory_space=pltpu.VMEM)
    return pl.pallas_call(
        body,
        out_shape=[jax.ShapeDtypeStruct((4, quarter), jnp.float32)] * 2,
        in_specs=[pl.BlockSpec(memory_space=pltpu.SMEM), vmem, vmem],
        out_specs=[vmem, vmem],
        scratch_shapes=[
            pltpu.VMEM((2, length, LANES), jnp.float32),
            pltpu.VMEM((2, count, LANES), jnp.float32),
            pltpu.VMEM((2, count, LANES), jnp.float32),
            pltpu.VMEM((length, LANES), jnp.float32),
            pltpu.VMEM((length, LANES), jnp.float32),
            pltpu.VMEM((length, LANES), jnp.float32),
            pltpu.VMEM((length, LANES), jnp.float32),
            pltpu.VMEM((2 * count, wide), jnp.bfloat16),
            pltpu.VMEM((2 * count, wide), jnp.bfloat16),
            pltpu.VMEM((count, count), jnp.float32),
            pltpu.VMEM((quarter, count), jnp.float32),
            pltpu.VMEM((quarter, count // 2), jnp.float32),
        ],
        compiler_params=pltpu.CompilerParams(vmem_limit_bytes=40 << 20),
    )(info, near, other)


def on_device(blocks, chans, series, tail, excl):
    count = series.shape[1]
    width = tail.shape[1]
    block = lax.axis_index("tm")
    chan = lax.axis_index("chan")
    both = ("tm", "chan")
    places = [(b, c) for b in range(blocks) for c in range(chans)]

    def shifted(value, reach):
        pairs = [
            ((b + reach(c)) * chans + c, b * chans + c)
            for b, c in places
            if 0 <= b + reach(c) < blocks
        ]
        return lax.ppermute(value, both, pairs)

    def swapped(value):
        return lax.ppermute(value, "chan", [(c, chans - 1 - c) for c in range(chans)])

    head = shifted(series[:, : width + 1], lambda c: 1)
    head = jnp.where(block == blocks - 1, jnp.pad(tail, ((0, 0), (0, 1))), head)
    extended = jnp.concatenate([series, head], axis=1)
    near = jnp.concatenate([extended, swapped(extended)], axis=0)
    other = shifted(near, lambda c: chans - c)
    shift = chans - chan
    info = jnp.stack([excl[0], chan, shift, (block + shift < blocks).astype(jnp.int32)])
    own, away = scores(info, near, other, count)
    home = shifted(away, lambda c: c - chans)
    best = jnp.minimum(own, jnp.where(block - shift >= 0, home, CEILING))
    return jnp.minimum(best, swapped(best)).reshape(count)


def solution(mesh):
    placed = (P("chan", "tm"), P("chan", None), P())
    run = functools.partial(on_device, mesh.shape["tm"], mesh.shape["chan"])
    return jax.shard_map(run, mesh=mesh, in_specs=placed, out_specs=P("tm"), check_vma=False)
```

time: 511 us -> 43 us (0.08)
  local copies, waits for them, and re-layouts: 240 us -> 0.79 us
  waiting for transfers between devices: 224 us -> 15.6 us
  between operations: 14.2 us -> 0.71 us
  Pallas kernels: 0 us -> 13.2 us
  other arithmetic: 12.6 us -> 1.41 us
  matrix products: 10.1 us -> 0 us
    gather x2 -> x0, local copies, waits for them, and re-layouts: 238 us -> none  [normalize(): windows = extended[:, starts]]
    ppermute x5, waiting for transfers between devices: 137 us -> 15.6 us  [the longest x3 9.64 us: shifted(): return lax.ppermute(value, both, pairs)]
    psum x1 -> x0, waiting for transfers between devices: 87.3 us -> none  [summed(): total = lax.psum(correlate(query, right), 'chan')]
    pallas_call x0 -> x1, Pallas kernels: none -> 13.2 us  [scores(): pl.pallas_call(body, out_shape=[jax.ShapeDtypeStruct((4, quarter), jnp.fl...]
    dot_general x3 -> x0, matrix products: 10.1 us -> none  [correlate(): lax.dot_general(left, right, (((0, 1), (0, 1)), ((), ())), preferred_elem...]
    reduce_sum x2 -> x0, other arithmetic: 6.18 us -> none  [the longest x1 4.74 us: normalize(): center = jnp.mean(windows, axis=1, keepdims=True)]
  transfers between devices with their start and end apart: 6 -> 5, of which waited for: 5 -> 5; matrix products, arithmetic and copies ran while one was open for 1% -> 0% of each run, Pallas kernels for 0% -> 0%
where the time goes in v1:
time: 43 us; the launch traced here: 42.7 us
  waiting for transfers between devices  15.6 us (36%)
  Pallas kernels  13.2 us (31%)
  starting transfers between devices  11 us (26%)
  other arithmetic  1.41 us (3%)
  local copies, waits for them, and re-layouts  0.79 us (2%)
  between operations  0.71 us (2%)
    pallas_call x1, Pallas kernels, scores(): pl.pallas_call(body, out_shape=[jax.ShapeDtypeStruct((4, quarter), jnp.fl...  13.2 us
    ppermute x3, waiting for transfers between devices, shifted(): return lax.ppermute(value, both, pairs)  9.64 us
    ppermute x3, starting transfers between devices, shifted(): return lax.ppermute(value, both, pairs)  7.91 us
    ppermute x2, waiting for transfers between devices, swapped(): lax.ppermute(value, 'chan', [(c, chans - 1 - c) for c in range(chans)])  6 us
    ppermute x2, starting transfers between devices, swapped(): lax.ppermute(value, 'chan', [(c, chans - 1 - c) for c in range(chans)])  3.06 us
  transfers between devices with their start and end apart: 5, of which 5 were waited for; matrix products, arithmetic and copies ran while one was open for 0% of the time, Pallas kernels for 0%

profile of v1, /device:TPU:0, one launch (start us, length us, event | category | flops | bytes accessed | tf_op | source)
XLA Modules:
  0.0 42.7 jit_solution(7010480606588204130)
XLA Ops:
  0.0 0.0 copy-start
  0.0 0.8 %slice.3 = f32[32,128]{1,0:T(8,128)S(1)} slice(f32[32,512]{1,0:T(8,128)} %param.3), slice={[0:32], [0:128]} | slice | bytes 32768 | tf_op jit(solution)/shard_map/slice | solution.py:202
  0.8 1.3 %collective-permute-start = (f32[32,128]{1,0:T(8,128)S(1)}, f32[32,128]{1,0:T(8,128)S(1)}, u32[]{:S(2)}, u32[]{:S(2)}) collective-permute-start(f32[32,128]{1,0:T(8,128)S(1)} %slice.3), channel_id=1, source_target_pairs={{2,0},{3,1},{4,2},{5,3},{6,4},{7,5},{8,6},{9,7},{10,8},{11,9},{12,... | collective-permute-start | bytes 49160 | tf_op jit(solution)/shard_map/ppermute | solution.py:197
  2.1 1.8 %collective-permute-done = f32[32,128]{1,0:T(8,128)S(1)} collective-permute-done((f32[32,128]{1,0:T(8,128)S(1)}, f32[32,128]{1,0:T(8,128)S(1)}, u32[]{:S(2)}, u32[]{:S(2)}) %collective-permute-start) | collective-permute-done | bytes 16416 | tf_op jit(solution)/shard_map/ppermute | solution.py:197
  3.9 0.7 %pad_select_fusion = f32[32,128]{1,0:T(8,128)S(1)} fusion(f32[32,128]{1,0:T(8,128)S(1)} %collective-permute-done, f32[32,127]{1,0:T(8,128)} %param.4, pred[]{:T(512)S(6)} %eq.3), kind=kLoop, calls=%fused_computation.2 | loop fusion | flops 4096 | bytes 49025 | tf_op jit(solution)/shard_map/jit(_where)/select_n | solution.py:203
  4.6 0.0 copy-done
  4.6 3.1 %collective-permute-start.1 = (f32[32,640]{1,0:T(8,128)S(1)}, f32[32,640]{1,0:T(8,128)S(1)}, u32[]{:S(2)}, u32[]{:S(2)}) collective-permute-start(f32[32,640]{1,0:T(8,128)S(1)} %pad_maximum_fusion.1), channel_id=1, source_target_pairs={{0,1},{1,0},{2,3},{3,2},{4,5},{5,4},{6,7},{7,6},{8,9},{9,8},{10,11... | collective-permute-start | bytes 245768 | tf_op jit(solution)/shard_map/ppermute | solution.py:200
  7.7 2.4 %collective-permute-done.1 = f32[32,640]{1,0:T(8,128)S(1)} collective-permute-done((f32[32,640]{1,0:T(8,128)S(1)}, f32[32,640]{1,0:T(8,128)S(1)}, u32[]{:S(2)}, u32[]{:S(2)}) %collective-permute-start.1) | collective-permute-done | bytes 81952 | tf_op jit(solution)/shard_map/ppermute | solution.py:200
  10.1 1.3 %collective-permute-start.2 = (f32[64,640]{1,0:T(8,128)S(1)}, f32[64,640]{1,0:T(8,128)S(1)}, u32[]{:S(2)}, u32[]{:S(2)}) collective-permute-start(f32[64,640]{1,0:T(8,128)S(1)} %pad_maximum_fusion.near), channel_id=1, source_target_pairs={{4,0},{3,1},{6,2},{5,3},{8,4},{7,5},{10,6},{9,7},{12,8},{11,9},{14... | collective-permute-start | bytes 491528 | tf_op jit(solution)/shard_map/ppermute | solution.py:197
  12.1 0.1 pad_add_fusion.info
  12.1 6.6 %collective-permute-done.2.other = f32[64,640]{1,0:T(8,128)S(1)} collective-permute-done((f32[64,640]{1,0:T(8,128)S(1)}, f32[64,640]{1,0:T(8,128)S(1)}, u32[]{:S(2)}, u32[]{:S(2)}) %collective-permute-start.2) | collective-permute-done | bytes 163872 | tf_op jit(solution)/shard_map/ppermute | solution.py:197
  18.7 13.2 %shard_map.37 = (f32[4,128]{1,0:T(4,128)S(1)}, f32[4,128]{1,0:T(4,128)S(1)}) custom-call(s32[4]{0:T(128)S(1)} %pad_add_fusion.info, f32[64,640]{1,0:T(8,128)S(1)} %pad_maximum_fusion.near, f32[64,640]{1,0:T(8,128)S(1)} %collective-permute-done.2.other), custom_call_target="tpu_custom_call" | custom-call | tf_op jit(solution)/shard_map/pallas_call | solution.py:160
  31.9 5.3 %collective-permute-start.3 = (f32[4,128]{1,0:T(4,128)S(1)}, f32[4,128]{1,0:T(4,128)S(1)}, u32[]{:S(2)}, u32[]{:S(2)}) collective-permute-start(f32[4,128]{1,0:T(4,128)S(1)} %get-tuple-element.8), channel_id=1, source_target_pairs={{1,3},{0,4},{3,5},{2,6},{5,7},{4,8},{7,9},{6,10},{9,11},{8,12},{11... | collective-permute-start | bytes 6152 | tf_op jit(solution)/shard_map/ppermute | solution.py:197
  37.3 1.3 %collective-permute-done.3 = f32[4,128]{1,0:T(4,128)S(1)} collective-permute-done((f32[4,128]{1,0:T(4,128)S(1)}, f32[4,128]{1,0:T(4,128)S(1)}, u32[]{:S(2)}, u32[]{:S(2)}) %collective-permute-start.3) | collective-permute-done | bytes 2080 | tf_op jit(solution)/shard_map/ppermute | solution.py:197
  38.6 0.0 collective-permute-start.4
  38.6 3.6 %collective-permute-done.4 = f32[4,128]{1,0:T(4,128)S(1)} collective-permute-done((f32[4,128]{1,0:T(4,128)S(1)}, f32[4,128]{1,0:T(4,128)S(1)}, u32[]{:S(2)}, u32[]{:S(2)}) %collective-permute-start.4) | collective-permute-done | bytes 2080 | tf_op jit(solution)/shard_map/ppermute | solution.py:200
  42.2 0.6 %minimum_bitcast_fusion = f32[512]{0:T(512)} fusion(f32[4,128]{1,0:T(4,128)S(1)} %select_minimum_fusion, f32[4,128]{1,0:T(4,128)S(1)} %collective-permute-done.4), kind=kLoop, calls=%fused_computation.3 | loop fusion | flops 512 | bytes 6144 | tf_op jit(solution)/shard_map/reshape | solution.py:212
  (3 shorter events, 0.0 us)
Async XLA Ops:
  0.0 4.6 %copy-start = (f32[32,512]{1,0:T(8,128)S(1)}, f32[32,512]{1,0:T(8,128)}, u32[]{:S(2)}) copy-start(f32[32,512]{1,0:T(8,128)} %param.3) | copy-start | bytes 196612
  0.8 3.1 %collective-permute-start = (f32[32,128]{1,0:T(8,128)S(1)}, f32[32,128]{1,0:T(8,128)S(1)}, u32[]{:S(2)}, u32[]{:S(2)}) collective-permute-start(f32[32,128]{1,0:T(8,128)S(1)} %slice.3), channel_id=1, source_target_pairs={{2,0},{3,1},{4,2},{5,3},{6,4},{7,5},{8,6},{9,7},{10,8},{11,9},{12,... | collective-permute-start | bytes 49160 | tf_op jit(solution)/shard_map/ppermute | solution.py:197
  4.6 5.5 %collective-permute-start.1 = (f32[32,640]{1,0:T(8,128)S(1)}, f32[32,640]{1,0:T(8,128)S(1)}, u32[]{:S(2)}, u32[]{:S(2)}) collective-permute-start(f32[32,640]{1,0:T(8,128)S(1)} %pad_maximum_fusion.1), channel_id=1, source_target_pairs={{0,1},{1,0},{2,3},{3,2},{4,5},{5,4},{6,7},{7,6},{8,9},{9,8},{10,11... | collective-permute-start | bytes 245768 | tf_op jit(solution)/shard_map/ppermute | solution.py:200
  10.1 8.6 %collective-permute-start.2 = (f32[64,640]{1,0:T(8,128)S(1)}, f32[64,640]{1,0:T(8,128)S(1)}, u32[]{:S(2)}, u32[]{:S(2)}) collective-permute-start(f32[64,640]{1,0:T(8,128)S(1)} %pad_maximum_fusion.near), channel_id=1, source_target_pairs={{4,0},{3,1},{6,2},{5,3},{8,4},{7,5},{10,6},{9,7},{12,8},{11,9},{14... | collective-permute-start | bytes 491528 | tf_op jit(solution)/shard_map/ppermute | solution.py:197
  31.9 6.6 %collective-permute-start.3 = (f32[4,128]{1,0:T(4,128)S(1)}, f32[4,128]{1,0:T(4,128)S(1)}, u32[]{:S(2)}, u32[]{:S(2)}) collective-permute-start(f32[4,128]{1,0:T(4,128)S(1)} %get-tuple-element.8), channel_id=1, source_target_pairs={{1,3},{0,4},{3,5},{2,6},{5,7},{4,8},{7,9},{6,10},{9,11},{8,12},{11... | collective-permute-start | bytes 6152 | tf_op jit(solution)/shard_map/ppermute | solution.py:197
  38.6 3.6 %collective-permute-start.4 = (f32[4,128]{1,0:T(4,128)S(1)}, f32[4,128]{1,0:T(4,128)S(1)}, u32[]{:S(2)}, u32[]{:S(2)}) collective-permute-start(f32[4,128]{1,0:T(4,128)S(1)} %select_minimum_fusion), channel_id=1, source_target_pairs={{0,1},{1,0},{2,3},{3,2},{4,5},{5,4},{6,7},{7,6},{8,9},{9,8},{10,11... | collective-permute-start | bytes 6152 | tf_op jit(solution)/shard_map/ppermute | solution.py:200

commit v2 on v1

v2 whole, which is shorter than its diff:
```python
import functools
import math

import jax
import jax.numpy as jnp
from jax import lax
from jax.experimental import pallas as pl
from jax.experimental.pallas import tpu as pltpu
from jax.sharding import PartitionSpec as P

EPSILON = 1e-05
CEILING = 4.0
FLOOR = 1.0 - CEILING
LANES = 128
STEPS = (16, 4)


def transposed(value, target):
    length = value.shape[1]
    half = LANES // 2
    ahead = pltpu.roll(value, length - half, 1)
    for start in range(0, length, LANES):
        stop = start + LANES
        both = jnp.concatenate([value[:, start:stop], ahead[:, start:stop]], axis=0)
        target[start:stop, :] = both.T


def statistics(samples, sums, moments, mean, scale, channels):
    count = mean.shape[0]
    window = samples.shape[0] - count
    half = window // 2
    current = samples
    size = 1
    level = 0
    while size < half:
        rows = -(-(count + half - 2 * size) // 8) * 8
        for start in range(0, rows, 64):
            stop = min(start + 64, rows)
            here = current[start:stop, :]
            there = current[start + size : stop + size, :]
            gap = here - there
            square = gap * gap
            if size > 1:
                old = moments[level % 2]
                square += 2.0 * (old[start:stop, :] + old[start + size : stop + size, :])
            sums[(level + 1) % 2][start:stop, :] = here + there
            moments[(level + 1) % 2][start:stop, :] = square
        level += 1
        current = sums[level % 2]
        size *= 2
    for start in range(0, count, 64):
        here = current[start : start + 64, :]
        there = pltpu.roll(here, LANES // 2, 1)
        gap = here - there
        old = moments[level % 2][start : start + 64, :]
        total = gap * gap + 2.0 * (old + pltpu.roll(old, LANES // 2, 1))
        mean[start : start + 64, :] = (here + there) * (1.0 / window)
        spread = total * (1.0 / (window * window))
        scale[start : start + 64, :] = lax.rsqrt(spread + EPSILON) * (
            1.0 / math.sqrt(window * channels)
        )


def contract(left, right):
    return lax.dot_general(
        left, right, (((1,), (1,)), ((), ())), preferred_element_type=jnp.float32
    )


def fill(samples, means, scales, zed, row, step, width):
    for start in range(0, means.shape[0], 16):
        mean = means[start : start + 16, :]
        scale = scales[start : start + 16, :]
        for inner in range(0, width, 2):
            parts = [
                (samples[pl.ds(step + (start + inner + side), 16), :] - mean) * scale
                for side in range(2)
            ]
            zed[row + start : row + start + 16, inner * LANES : (inner + 2) * LANES] = (
                jnp.concatenate(parts, axis=1).astype(jnp.bfloat16)
            )


def streamed(steps, build, multiply):
    width, blocks = steps
    build(0, 0, width)

    def pair(index, carry):
        for slot in range(2):
            build(1 - slot, (2 * index + slot + 1) * width, width)
            multiply(slot, width)
        return carry

    lax.fori_loop(0, blocks // 2, pair, 0)


def gap_of(shape, row_start, column_start):
    rows = lax.broadcasted_iota(jnp.int32, shape, 0) + row_start
    columns = lax.broadcasted_iota(jnp.int32, shape, 1) + column_start
    return rows - columns


def rows_best(value):
    best = value[:, :LANES]
    for start in range(LANES, value.shape[1], LANES):
        best = jnp.maximum(best, value[:, start : start + LANES])
    return jnp.max(best.T, axis=0, keepdims=True)


def own_body(info, near, head, tail, samples, means, scales, sums_a, sums_b, moments_a, moments_b):
    last = jnp.where(info[4] > 0, tail[...], head[...])
    transposed(jnp.concatenate([near[...], last], axis=1), samples)
    statistics(
        samples, (sums_a, sums_b), (moments_a, moments_b), means, scales, near.shape[0]
    )


def cross_body(
    info, samples, means, scales, other, head, tail, away_out, own_out,
    samples_b, means_b, scales_b, sums_a, sums_b, moments_a, moments_b,
    zed_a, zed_b, left, right,
):
    count = means.shape[0]
    half, quarter = count // 2, count // 4
    limit, chan, shift, valid = info[0], info[1], info[2], info[3]
    last = jnp.where(info[5] > 0, tail[...], head[...])
    transposed(jnp.concatenate([other[...], last], axis=1), samples_b)
    statistics(
        samples_b, (sums_a, sums_b), (moments_a, moments_b), means_b, scales_b, other.shape[0]
    )
    zeds = (zed_a, zed_b)
    starts = [
        pl.multiple_of(chan * quarter, quarter),
        pl.multiple_of(half + chan * quarter, quarter),
    ]

    def build(slot, step, width):
        zed = zeds[slot]
        fill(samples, means, scales, zed, 0, step, width)
        fill(samples_b, means_b, scales_b, zed, count, step, width)
        for index, start in enumerate(starts):
            row = 2 * count + index * quarter
            zed[row : row + quarter, :] = zed[pl.ds(start, quarter), :]

    def multiply(slot, width):
        zed = zeds[slot]
        left[...] += contract(zed[count : 2 * count + quarter, :], zed[:half, :])
        right[...] += contract(zed[count : 2 * count + half, :], zed[half:count, :])

    left[...] = jnp.zeros_like(left)
    right[...] = jnp.zeros_like(right)
    streamed(STEPS, build, multiply)

    bests = []
    columns = []
    for index, (block, column) in enumerate(((left, 0), (right, half))):
        value = block[:count, :]
        far = (gap_of(value.shape, shift * count, column) >= limit) & (valid > 0)
        value = jnp.where(far, value, FLOOR)
        bests.append(value)
        columns.append(jnp.max(value, axis=0, keepdims=True))
    far = jnp.maximum(bests[0], bests[1])
    for index in range(4):
        rows = slice(index * quarter, (index + 1) * quarter)
        away_out[index : index + 1, :] = 1.0 - rows_best(far[rows, :])
    lines = []
    for index, start in enumerate(starts):
        rows = slice(count + index * quarter, count + (index + 1) * quarter)
        best = None
        for block, column in ((left, 0), (right, half))[index:]:
            value = block[rows, :]
            value = jnp.where(jnp.abs(gap_of(value.shape, start, column)) >= limit, value, FLOOR)
            side = column // half
            columns[side] = jnp.maximum(columns[side], jnp.max(value, axis=0, keepdims=True))
            best = value if best is None else jnp.maximum(best, value)
        lines.append(rows_best(best))
    for index in range(4):
        place = slice((index % 2) * quarter, (index % 2 + 1) * quarter)
        line = jnp.where(chan == index % 2, lines[index // 2], FLOOR)
        own_out[index : index + 1, :] = 1.0 - jnp.maximum(columns[index // 2][:, place], line)


SMEM = pl.BlockSpec(memory_space=pltpu.SMEM)
VMEM = pl.BlockSpec(memory_space=pltpu.VMEM)


def sized(*shape, dtype=jnp.float32):
    return jax.ShapeDtypeStruct(shape, dtype)


def prepare(info, near, head, tail):
    channels, count = near.shape
    length = count + head.shape[1]
    return pl.pallas_call(
        own_body,
        out_shape=[sized(length, LANES), sized(count, LANES), sized(count, LANES)],
        in_specs=[SMEM, VMEM, VMEM, VMEM],
        out_specs=[VMEM] * 3,
        scratch_shapes=[pltpu.VMEM((length, LANES), jnp.float32)] * 4,
        compiler_params=pltpu.CompilerParams(vmem_limit_bytes=8 << 20),
        cost_estimate=pl.CostEstimate(flops=4_000_000, bytes_accessed=1 << 21, transcendentals=0),
    )(info, near, head, tail)


def crossed(info, own, other, head, tail):
    channels, count = other.shape
    length = count + head.shape[1]
    quarter = count // 4
    wide = STEPS[0] * LANES
    flops = 2 * count * count * channels * (length - count)
    return pl.pallas_call(
        cross_body,
        out_shape=[sized(4, quarter)] * 2,
        in_specs=[SMEM] + [VMEM] * 6,
        out_specs=[VMEM] * 2,
        scratch_shapes=[
            pltpu.VMEM((length, LANES), jnp.float32),
            pltpu.VMEM((count, LANES), jnp.float32),
            pltpu.VMEM((count, LANES), jnp.float32),
            *[pltpu.VMEM((length, LANES), jnp.float32)] * 4,
            *[pltpu.VMEM((2 * count + count // 2, wide), jnp.bfloat16)] * 2,
            pltpu.VMEM((count + quarter, count // 2), jnp.float32),
            pltpu.VMEM((count + count // 2, count // 2), jnp.float32),
        ],
        compiler_params=pltpu.CompilerParams(vmem_limit_bytes=32 << 20),
        cost_estimate=pl.CostEstimate(flops=flops, bytes_accessed=1 << 21, transcendentals=0),
    )(info, *own, other, head, tail)


def on_device(blocks, chans, series, tail, excl):
    count = series.shape[1]
    window = tail.shape[1] + 1
    block = lax.axis_index("tm")
    chan = lax.axis_index("chan")
    axes = ("tm", "chan")
    places = [(b, c) for b in range(blocks) for c in range(chans)]

    def shifted(value, reach):
        pairs = [
            ((b + reach(c)) * chans + c, b * chans + c)
            for b, c in places
            if 0 <= b + reach(c) < blocks
        ]
        return lax.ppermute(value, axes, pairs)

    def swapped(value):
        return lax.ppermute(value, "chan", [(c, chans - 1 - c) for c in range(chans)])

    shift = chans - chan
    flags = [block + shift < blocks, block == blocks - 1, block + shift == blocks - 1]
    info = jnp.stack([excl[0], chan, shift] + [flag.astype(jnp.int32) for flag in flags])
    spare = jnp.zeros((series.shape[0], 1), series.dtype)
    padded = jnp.concatenate([series, tail, spare], axis=1)
    partner = swapped(padded)
    near = jnp.concatenate([padded[:, :count], partner[:, :count]], axis=0)
    ending = jnp.concatenate([padded[:, count:], partner[:, count:]], axis=0)
    with jax.named_scope("block"):
        other = shifted(near, lambda c: chans - c)
    with jax.named_scope("next_head"):
        head = shifted(near[:, :window], lambda c: 1)
    with jax.named_scope("far_head"):
        other_head = shifted(near[:, :window], lambda c: chans + 1 - c)
    own = prepare(info, near, head, ending)
    away, best = crossed(info, own, other, other_head, ending)
    home = shifted(away, lambda c: c - chans)
    best = jnp.minimum(best, jnp.where(block - shift >= 0, home, CEILING))
    return jnp.minimum(best, swapped(best)).reshape(count)


def solution(mesh):
    placed = (P("chan", "tm"), P("chan", None), P())
    run = functools.partial(on_device, mesh.shape["tm"], mesh.shape["chan"])
    return jax.shard_map(run, mesh=mesh, in_specs=placed, out_specs=P("tm"), check_vma=False)
```

time: 43 us -> 37.8 us (0.88)
  waiting for transfers between devices: 15.6 us -> 10.9 us
  Pallas kernels: 13.2 us -> 12.1 us
  starting transfers between devices: 11 us -> 11.9 us
  local copies, waits for them, and re-layouts: 0.79 us -> 0.18 us
    ppermute x3 -> x4, waiting for transfers between devices: 9.64 us -> 5.57 us  [shifted(): return lax.ppermute(value, axes, pairs)]
    pallas_call x1 -> x2, Pallas kernels: 13.2 us -> 12.1 us  [the longest x1 10.8 us: crossed(): pl.pallas_call(cross_body, out_shape=[sized(4, quarter)] * 2, in_specs=[S...]
    ppermute x3 -> x4, starting transfers between devices: 7.91 us -> 8.8 us  [shifted(): return lax.ppermute(value, axes, pairs)]
    concatenate x2 -> x4, other arithmetic: 0.02 us -> 0.89 us  [the longest x1 0.87 us: on_device(): padded = jnp.concatenate([series, tail, spare], axis=1)]
    slice x1 -> x2, local copies, waits for them, and re-layouts: 0.79 us -> 0.01 us  [the longest x1 0.01 us: on_device(): near = jnp.concatenate([padded[:, :count], partner[:, :count]], axis=0)]
    select_n x1 -> x0, other arithmetic: 0.72 us -> none  [on_device(): head = jnp.where(block == blocks - 1, jnp.pad(tail, ((0, 0), (0, 1))), head)]
    ppermute x2, waiting for transfers between devices: 6 us -> 5.29 us  [swapped(): lax.ppermute(value, 'chan', [(c, chans - 1 - c) for c in range(chans)])]
  transfers between devices with their start and end apart: 5 -> 6, of which waited for: 5 -> 5; matrix products, arithmetic and copies ran while one was open for 0% -> 0% of each run, Pallas kernels for 0% -> 3%
where the time goes in v2:
time: 37.8 us; the launch traced here: 37.2 us
  Pallas kernels  12.1 us (32%)
  starting transfers between devices  11.9 us (31%)
  waiting for transfers between devices  10.9 us (29%)
  other arithmetic  1.47 us (4%)
  between operations  0.76 us (2%)
    pallas_call x1, Pallas kernels, crossed(): pl.pallas_call(cross_body, out_shape=[sized(4, quarter)] * 2, in_specs=[S...  10.8 us
    ppermute x4, starting transfers between devices, shifted(): return lax.ppermute(value, axes, pairs)  8.8 us
    ppermute x4, waiting for transfers between devices, shifted(): return lax.ppermute(value, axes, pairs)  5.57 us
    ppermute x2, waiting for transfers between devices, swapped(): lax.ppermute(value, 'chan', [(c, chans - 1 - c) for c in range(chans)])  5.29 us
    ppermute x2, starting transfers between devices, swapped(): lax.ppermute(value, 'chan', [(c, chans - 1 - c) for c in range(chans)])  3.06 us
    pallas_call x1, Pallas kernels, prepare(): pl.pallas_call(own_body, out_shape=[sized(length, LANES), sized(count, LA...  1.25 us
    concatenate x1, other arithmetic, on_device(): padded = jnp.concatenate([series, tail, spare], axis=1)  0.87 us
  transfers between devices with their start and end apart: 6, of which 5 were waited for; matrix products, arithmetic and copies ran while one was open for 0% of the time, Pallas kernels for 3%

profile of v2, /device:TPU:0, one launch (start us, length us, event | category | flops | bytes accessed | tf_op | source)
XLA Modules:
  0.0 37.2 jit_solution(4747959628356817892)
XLA Ops:
  0.0 0.1 pad.7.clone
  0.1 0.9 %maximum_maximum_fusion = f32[32,640]{1,0:T(8,128)S(1)} fusion(f32[32,127]{1,0:T(8,128)} %param.4, f32[32,512]{1,0:T(8,128)} %param.3, f32[640]{0:T(1024)S(1)} %pad.7.clone), kind=kLoop, calls=%fused_computation.3 | loop fusion | flops 40960 | bytes 166272 | tf_op jit(solution)/shard_map/concatenate | solution.py:253
  0.9 3.1 %collective-permute-start = (f32[32,640]{1,0:T(8,128)S(1)}, f32[32,640]{1,0:T(8,128)S(1)}, u32[]{:S(2)}, u32[]{:S(2)}) collective-permute-start(f32[32,640]{1,0:T(8,128)S(1)} %maximum_maximum_fusion), channel_id=1, source_target_pairs={{0,1},{1,0},{2,3},{3,2},{4,5},{5,4},{6,7},{7,6},{8,9},{9,8},{10,11... | collective-permute-start | bytes 245768 | tf_op jit(solution)/shard_map/ppermute | solution.py:247
  4.7 0.1 stack.35.info
  4.7 0.0 copy-start
  4.7 1.7 %collective-permute-done = f32[32,640]{1,0:T(8,128)S(1)} collective-permute-done((f32[32,640]{1,0:T(8,128)S(1)}, f32[32,640]{1,0:T(8,128)S(1)}, u32[]{:S(2)}, u32[]{:S(2)}) %collective-permute-start) | collective-permute-done | bytes 81952 | tf_op jit(solution)/shard_map/ppermute | solution.py:247
  6.5 0.0 copy-done
  6.5 1.3 %collective-permute-start.2 = (f32[64,512]{1,0:T(8,128)S(1)}, f32[64,512]{1,0:T(8,128)S(1)}, u32[]{:S(2)}, u32[]{:S(2)}) collective-permute-start(f32[64,512]{1,0:T(8,128)S(1)} %pad_maximum_fusion.near), channel_id=1, source_target_pairs={{4,0},{3,1},{6,2},{5,3},{8,4},{7,5},{10,6},{9,7},{12,8},{11,9},{14... | collective-permute-start | bytes 393224 | tf_op jit(solution)/shard_map/block/ppermute | solution.py:244
  7.8 0.0 copy-start.1
  7.8 1.3 %collective-permute-start.1 = (f32[64,128]{1,0:T(8,128)S(1)}, f32[64,128]{1,0:T(8,128)S(1)}, u32[]{:S(2)}, u32[]{:S(2)}) collective-permute-start(f32[64,128]{1,0:T(8,128)S(1)} %fusion), channel_id=1, source_target_pairs={{2,0},{3,1},{4,2},{5,3},{6,4},{7,5},{8,6},{9,7},{10,8},{11,9},{12,... | collective-permute-start | bytes 98312 | tf_op jit(solution)/shard_map/next_head/ppermute | solution.py:244
  9.1 1.3 %collective-permute-start.3 = (f32[64,128]{1,0:T(8,128)S(1)}, f32[64,128]{1,0:T(8,128)S(1)}, u32[]{:S(2)}, u32[]{:S(2)}) collective-permute-start(f32[64,128]{1,0:T(8,128)S(1)} %fusion), channel_id=1, source_target_pairs={{6,0},{5,1},{8,2},{7,3},{10,4},{9,5},{12,6},{11,7},{14,8},{13,9},{... | collective-permute-start | bytes 98312 | tf_op jit(solution)/shard_map/far_head/ppermute | solution.py:244
  10.4 0.0 copy-done.1
  10.4 0.5 %collective-permute-done.1.head = f32[64,128]{1,0:T(8,128)S(1)} collective-permute-done((f32[64,128]{1,0:T(8,128)S(1)}, f32[64,128]{1,0:T(8,128)S(1)}, u32[]{:S(2)}, u32[]{:S(2)}) %collective-permute-start.1) | collective-permute-done | bytes 32800 | tf_op jit(solution)/shard_map/next_head/ppermute | solution.py:244
  10.9 1.3 %shard_map.37 = (f32[640,128]{1,0:T(8,128)S(1)}, f32[512,128]{1,0:T(8,128)S(1)}, f32[512,128]{1,0:T(8,128)S(1)}) custom-call(s32[6]{0:T(128)S(1)} %stack.35.info, f32[64,512]{1,0:T(8,128)S(1)} %pad_maximum_fusion.near, f32[64,128]{1,0:T(8,128)S(1)} %collective-permute-done.1.head, f32[64,128]{1,0:T(8,128)S(1)} %select_maximum_fusion.tail), custom_call_target="tpu_custom_call" | custom-call | flops 4000000 | bytes 2097152 | tf_op jit(solution)/shard_map/pallas_call | solution.py:194
  12.2 3.8 %collective-permute-done.3.head = f32[64,128]{1,0:T(8,128)S(1)} collective-permute-done((f32[64,128]{1,0:T(8,128)S(1)}, f32[64,128]{1,0:T(8,128)S(1)}, u32[]{:S(2)}, u32[]{:S(2)}) %collective-permute-start.3) | collective-permute-done | bytes 32800 | tf_op jit(solution)/shard_map/far_head/ppermute | solution.py:244
  16.0 0.0 collective-permute-done.2.other
  16.0 10.8 %shard_map.38 = (f32[4,128]{1,0:T(4,128)S(1)}, f32[4,128]{1,0:T(4,128)S(1)}) custom-call(s32[6]{0:T(128)S(1)} %stack.35.info, f32[640,128]{1,0:T(8,128)S(1)} %get-tuple-element.10.samples, f32[512,128]{1,0:T(8,128)S(1)} %get-tuple-element.11.means, f32[512,128]{1,0:T(8,128)S(1)} %get-tuple-element.12.scales, f32[64,512]{1,0:T(8,128)S(1)} %collective-permute-done.2.other, ...), custom_call_target="tpu_custom_call" | custom-call | flops 4294967296 | bytes 2097152 | tf_op jit(solution)/shard_map/pallas_call | solution.py:211
  26.8 4.9 %collective-permute-start.4 = (f32[4,128]{1,0:T(4,128)S(1)}, f32[4,128]{1,0:T(4,128)S(1)}, u32[]{:S(2)}, u32[]{:S(2)}) collective-permute-start(f32[4,128]{1,0:T(4,128)S(1)} %get-tuple-element.14), channel_id=1, source_target_pairs={{1,3},{0,4},{3,5},{2,6},{5,7},{4,8},{7,9},{6,10},{9,11},{8,12},{11... | collective-permute-start | bytes 6152 | tf_op jit(solution)/shard_map/ppermute | solution.py:244
  31.8 1.3 %collective-permute-done.4 = f32[4,128]{1,0:T(4,128)S(1)} collective-permute-done((f32[4,128]{1,0:T(4,128)S(1)}, f32[4,128]{1,0:T(4,128)S(1)}, u32[]{:S(2)}, u32[]{:S(2)}) %collective-permute-start.4) | collective-permute-done | bytes 2080 | tf_op jit(solution)/shard_map/ppermute | solution.py:244
  33.1 0.0 collective-permute-start.5
  33.1 3.6 %collective-permute-done.5 = f32[4,128]{1,0:T(4,128)S(1)} collective-permute-done((f32[4,128]{1,0:T(4,128)S(1)}, f32[4,128]{1,0:T(4,128)S(1)}, u32[]{:S(2)}, u32[]{:S(2)}) %collective-permute-start.5) | collective-permute-done | bytes 2080 | tf_op jit(solution)/shard_map/ppermute | solution.py:247
  36.6 0.6 %minimum_bitcast_fusion = f32[512]{0:T(512)} fusion(f32[4,128]{1,0:T(4,128)S(1)} %select_minimum_fusion, f32[4,128]{1,0:T(4,128)S(1)} %collective-permute-done.5), kind=kLoop, calls=%fused_computation.7 | loop fusion | flops 512 | bytes 6144 | tf_op jit(solution)/shard_map/reshape | solution.py:267
  (6 shorter events, 0.0 us)
Async XLA Ops:
  0.9 5.5 %collective-permute-start = (f32[32,640]{1,0:T(8,128)S(1)}, f32[32,640]{1,0:T(8,128)S(1)}, u32[]{:S(2)}, u32[]{:S(2)}) collective-permute-start(f32[32,640]{1,0:T(8,128)S(1)} %maximum_maximum_fusion), channel_id=1, source_target_pairs={{0,1},{1,0},{2,3},{3,2},{4,5},{5,4},{6,7},{7,6},{8,9},{9,8},{10,11... | collective-permute-start | bytes 245768 | tf_op jit(solution)/shard_map/ppermute | solution.py:247
  4.7 1.7 %copy-start = (f32[32,512]{1,0:T(8,128)S(1)}, f32[32,512]{1,0:T(8,128)}, u32[]{:S(2)}) copy-start(f32[32,512]{1,0:T(8,128)} %param.3) | copy-start | bytes 196612
  6.5 9.5 %collective-permute-start.2 = (f32[64,512]{1,0:T(8,128)S(1)}, f32[64,512]{1,0:T(8,128)S(1)}, u32[]{:S(2)}, u32[]{:S(2)}) collective-permute-start(f32[64,512]{1,0:T(8,128)S(1)} %pad_maximum_fusion.near), channel_id=1, source_target_pairs={{4,0},{3,1},{6,2},{5,3},{8,4},{7,5},{10,6},{9,7},{12,8},{11,9},{14... | collective-permute-start | bytes 393224 | tf_op jit(solution)/shard_map/block/ppermute | solution.py:244
  7.8 2.6 %copy-start.1 = (f32[32,127]{1,0:T(8,128)S(1)}, f32[32,127]{1,0:T(8,128)}, u32[]{:S(2)}) copy-start(f32[32,127]{1,0:T(8,128)} %param.4) | copy-start | bytes 48772
  7.8 3.1 %collective-permute-start.1 = (f32[64,128]{1,0:T(8,128)S(1)}, f32[64,128]{1,0:T(8,128)S(1)}, u32[]{:S(2)}, u32[]{:S(2)}) collective-permute-start(f32[64,128]{1,0:T(8,128)S(1)} %fusion), channel_id=1, source_target_pairs={{2,0},{3,1},{4,2},{5,3},{6,4},{7,5},{8,6},{9,7},{10,8},{11,9},{12,... | collective-permute-start | bytes 98312 | tf_op jit(solution)/shard_map/next_head/ppermute | solution.py:244
  9.1 6.9 %collective-permute-start.3 = (f32[64,128]{1,0:T(8,128)S(1)}, f32[64,128]{1,0:T(8,128)S(1)}, u32[]{:S(2)}, u32[]{:S(2)}) collective-permute-start(f32[64,128]{1,0:T(8,128)S(1)} %fusion), channel_id=1, source_target_pairs={{6,0},{5,1},{8,2},{7,3},{10,4},{9,5},{12,6},{11,7},{14,8},{13,9},{... | collective-permute-start | bytes 98312 | tf_op jit(solution)/shard_map/far_head/ppermute | solution.py:244
  26.8 6.2 %collective-permute-start.4 = (f32[4,128]{1,0:T(4,128)S(1)}, f32[4,128]{1,0:T(4,128)S(1)}, u32[]{:S(2)}, u32[]{:S(2)}) collective-permute-start(f32[4,128]{1,0:T(4,128)S(1)} %get-tuple-element.14), channel_id=1, source_target_pairs={{1,3},{0,4},{3,5},{2,6},{5,7},{4,8},{7,9},{6,10},{9,11},{8,12},{11... | collective-permute-start | bytes 6152 | tf_op jit(solution)/shard_map/ppermute | solution.py:244
  33.1 3.6 %collective-permute-start.5 = (f32[4,128]{1,0:T(4,128)S(1)}, f32[4,128]{1,0:T(4,128)S(1)}, u32[]{:S(2)}, u32[]{:S(2)}) collective-permute-start(f32[4,128]{1,0:T(4,128)S(1)} %select_minimum_fusion), channel_id=1, source_target_pairs={{0,1},{1,0},{2,3},{3,2},{4,5},{5,4},{6,7},{7,6},{8,9},{9,8},{10,11... | collective-permute-start | bytes 6152 | tf_op jit(solution)/shard_map/ppermute | solution.py:247

commit v3 on v2

v3 whole, which is shorter than its diff:
```python
import functools
import math

import jax
import jax.numpy as jnp
from jax import lax
from jax.experimental import pallas as pl
from jax.experimental.pallas import tpu as pltpu
from jax.sharding import PartitionSpec as P


EPSILON = 1e-05
CEILING = 4.0
FLOOR = 1.0 - CEILING
LANES = 128
WIDTH = 16


def transposed(value, target):
    length = value.shape[1]
    half = LANES // 2
    ahead = pltpu.roll(value, length - half, 1)
    for start in range(0, length, LANES):
        stop = start + LANES
        both = jnp.concatenate([value[:, start:stop], ahead[:, start:stop]], axis=0)
        target[start:stop, :] = both.T


def statistics(samples, sums, moments, mean, scale, channels):
    count = mean.shape[0]
    window = samples.shape[0] - count
    half = window // 2
    current = samples
    size = 1
    level = 0
    while size < half:
        rows = -(-(count + half - 2 * size) // 8) * 8
        for start in range(0, rows, 64):
            stop = min(start + 64, rows)
            here = current[start:stop, :]
            there = current[start + size : stop + size, :]
            gap = here - there
            square = gap * gap
            if size > 1:
                old = moments[level % 2]
                square += 2.0 * (old[start:stop, :] + old[start + size : stop + size, :])
            sums[(level + 1) % 2][start:stop, :] = here + there
            moments[(level + 1) % 2][start:stop, :] = square
        level += 1
        current = sums[level % 2]
        size *= 2
    for start in range(0, count, 64):
        here = current[start : start + 64, :]
        there = pltpu.roll(here, LANES // 2, 1)
        gap = here - there
        old = moments[level % 2][start : start + 64, :]
        total = gap * gap + 2.0 * (old + pltpu.roll(old, LANES // 2, 1))
        mean[start : start + 64, :] = (here + there) * (1.0 / window)
        spread = total * (1.0 / (window * window))
        scale[start : start + 64, :] = lax.rsqrt(spread + EPSILON) * (
            1.0 / math.sqrt(window * channels)
        )


def contract(left, right):
    return lax.dot_general(
        left, right, (((1,), (1,)), ((), ())), preferred_element_type=jnp.float32
    )


def fill(samples, means, scales, zed, step, base):
    for start in range(0, means.shape[0], 16):
        mean = means[start : start + 16, :]
        scale = scales[start : start + 16, :]
        for inner in range(0, WIDTH, 2):
            parts = [
                (samples[pl.ds(step + (start + inner + side), 16), :] - mean) * scale
                for side in range(2)
            ]
            zed[start : start + 16, pl.ds(base + inner * LANES, 2 * LANES)] = (
                jnp.concatenate(parts, axis=1).astype(jnp.bfloat16)
            )


def block_of(index):
    return pl.multiple_of(index * (WIDTH * LANES), WIDTH * LANES)


def gap_of(shape, row_start, column_start):
    rows = lax.broadcasted_iota(jnp.int32, shape, 0) + row_start
    columns = lax.broadcasted_iota(jnp.int32, shape, 1) + column_start
    return rows - columns


def rows_best(value):
    best = value[:, :LANES]
    for start in range(LANES, value.shape[1], LANES):
        best = jnp.maximum(best, value[:, start : start + LANES])
    return jnp.max(best.T, axis=0, keepdims=True)


def own_body(
    info, near, head, tail, zed_out,
    samples, means, scales, sums_a, sums_b, moments_a, moments_b,
):
    last = jnp.where(info[4] > 0, tail[...], head[...])
    transposed(jnp.concatenate([near[...], last], axis=1), samples)
    statistics(
        samples, (sums_a, sums_b), (moments_a, moments_b), means, scales, near.shape[0]
    )

    def build(index, carry):
        fill(samples, means, scales, zed_out, index * WIDTH, block_of(index))
        return carry

    lax.fori_loop(0, zed_out.shape[1] // (WIDTH * LANES), build, 0)


def cross_body(
    info, mine, other, head, tail, away_out, part_out,
    samples, means, scales, sums_a, sums_b, moments_a, moments_b, zed_a, zed_b, cross,
):
    count = means.shape[0]
    quarter = count // 4
    limit, shift, valid = info[0], info[2], info[3]
    last = jnp.where(info[5] > 0, tail[...], head[...])
    transposed(jnp.concatenate([other[...], last], axis=1), samples)
    statistics(
        samples, (sums_a, sums_b), (moments_a, moments_b), means, scales, other.shape[0]
    )
    zeds = (zed_a, zed_b)
    cross[...] = jnp.zeros_like(cross)
    fill(samples, means, scales, zed_a, 0, 0)

    def pair(index, carry):
        for slot in range(2):
            block = 2 * index + slot
            cross[...] += contract(
                zeds[slot][...], mine[:, pl.ds(block_of(block), WIDTH * LANES)]
            )
            fill(samples, means, scales, zeds[1 - slot], (block + 1) * WIDTH, 0)
        return carry

    lax.fori_loop(0, mine.shape[1] // (2 * WIDTH * LANES), pair, 0)
    far = jnp.where(
        (gap_of(cross.shape, shift * count, 0) >= limit) & (valid > 0), cross[...], FLOOR
    )
    columns = jnp.max(far, axis=0, keepdims=True)
    for index in range(4):
        rows = slice(index * quarter, (index + 1) * quarter)
        away_out[index : index + 1, :] = 1.0 - rows_best(far[rows, :])
        part_out[index : index + 1, :] = columns[:, rows]


def pair_body(info, mine, part, own_out, stage_a, stage_b, pair):
    count = mine.shape[0]
    quarter = count // 4
    limit, chan = info[0], info[1]
    stages = (stage_a, stage_b)
    starts = [
        pl.multiple_of(chan * quarter, quarter),
        pl.multiple_of(2 * quarter + chan * quarter, quarter),
    ]
    pair[...] = jnp.zeros_like(pair)

    def step(index, carry):
        for slot in range(2):
            lanes = pl.ds(block_of(2 * index + slot), WIDTH * LANES)
            for place, start in enumerate(starts):
                stages[slot][place * quarter : (place + 1) * quarter, :] = mine[
                    pl.ds(start, quarter), lanes
                ]
            pair[...] += contract(mine[:, lanes], stages[slot][...])
        return carry

    lax.fori_loop(0, mine.shape[1] // (2 * WIDTH * LANES), step, 0)
    near = []
    for index, start in enumerate(starts):
        value = pair[:, index * quarter : (index + 1) * quarter]
        near.append(jnp.where(jnp.abs(gap_of(value.shape, 0, start)) >= limit, value, FLOOR))
    lines = [jnp.max(value, axis=0, keepdims=True) for value in near]
    both = jnp.maximum(near[0], near[1])
    for index in range(4):
        best = rows_best(both[index * quarter : (index + 1) * quarter, :])
        best = jnp.maximum(best, part[index : index + 1, :])
        line = jnp.where(chan == index % 2, lines[index // 2], FLOOR)
        own_out[index : index + 1, :] = 1.0 - jnp.maximum(best, line)


SMEM = pl.BlockSpec(memory_space=pltpu.SMEM)
VMEM = pl.BlockSpec(memory_space=pltpu.VMEM)


def sized(*shape, dtype=jnp.float32):
    return jax.ShapeDtypeStruct(shape, dtype)


def working(count, length):
    long, short = pltpu.VMEM((length, LANES), jnp.float32), pltpu.VMEM((count, LANES), jnp.float32)
    return [long, short, short, long, long, long, long]


def settings(flops):
    return dict(
        compiler_params=pltpu.CompilerParams(vmem_limit_bytes=16 << 20),
        cost_estimate=pl.CostEstimate(flops=flops, bytes_accessed=1 << 21, transcendentals=0),
    )


def prepare(info, near, head, tail):
    channels, count = near.shape
    window = head.shape[1]
    return pl.pallas_call(
        own_body,
        out_shape=sized(count, channels * window, dtype=jnp.bfloat16),
        in_specs=[SMEM, VMEM, VMEM, VMEM],
        out_specs=VMEM,
        scratch_shapes=working(count, count + window),
        **settings(count * channels * window * 100),
    )(info, near, head, tail)


def crossed(info, mine, other, head, tail):
    channels, count = other.shape
    window = head.shape[1]
    return pl.pallas_call(
        cross_body,
        out_shape=[sized(4, count // 4)] * 2,
        in_specs=[SMEM] + [VMEM] * 4,
        out_specs=[VMEM] * 2,
        scratch_shapes=[
            *working(count, count + window),
            *[pltpu.VMEM((count, WIDTH * LANES), jnp.bfloat16)] * 2,
            pltpu.VMEM((count, count), jnp.float32),
        ],
        **settings(2 * count * count * channels * window),
    )(info, mine, other, head, tail)


def paired(info, mine, part):
    count, depth = mine.shape
    return pl.pallas_call(
        pair_body,
        out_shape=sized(4, count // 4),
        in_specs=[SMEM] + [VMEM] * 2,
        out_specs=VMEM,
        scratch_shapes=[
            *[pltpu.VMEM((count // 2, WIDTH * LANES), jnp.bfloat16)] * 2,
            pltpu.VMEM((count, count // 2), jnp.float32),
        ],
        **settings(count * count * depth),
    )(info, mine, part)


def on_device(blocks, chans, series, tail, excl):
    return profile(blocks, chans, series, tail, excl)


def profile(blocks, chans, series, tail, excl):
    count = series.shape[1]
    window = tail.shape[1] + 1
    block = lax.axis_index("tm")
    chan = lax.axis_index("chan")
    axes = ("tm", "chan")
    places = [(b, c) for b in range(blocks) for c in range(chans)]

    def shifted(value, reach):
        pairs = [
            ((b + reach(c)) * chans + c, b * chans + c)
            for b, c in places
            if 0 <= b + reach(c) < blocks
        ]
        return lax.ppermute(value, axes, pairs)

    def swapped(value):
        return lax.ppermute(value, "chan", [(c, chans - 1 - c) for c in range(chans)])

    shift = chans - chan
    flags = [block + shift < blocks, block == blocks - 1, block + shift == blocks - 1]
    info = jnp.stack([excl[0], chan, shift] + [flag.astype(jnp.int32) for flag in flags])
    spare = jnp.zeros((series.shape[0], 1), series.dtype)
    padded = lax.optimization_barrier(jnp.concatenate([series, tail, spare], axis=1))
    partner = swapped(padded)
    near = jnp.concatenate([padded[:, :count], partner[:, :count]], axis=0)
    ending = jnp.concatenate([padded[:, count:], partner[:, count:]], axis=0)
    other = shifted(near, lambda c: chans - c)
    head = shifted(near[:, :window], lambda c: 1)
    other_head = shifted(near[:, :window], lambda c: chans + 1 - c)
    mine = prepare(info, near, head, ending)
    away, part = crossed(info, mine, other, other_head, ending)
    home = shifted(away, lambda c: c - chans)
    best = paired(info, mine, part)
    best = jnp.minimum(best, jnp.where(block - shift >= 0, home, CEILING))
    return jnp.minimum(best, swapped(best)).reshape(count)


def solution(mesh):
    placed = (P("chan", "tm"), P("chan", None), P())
    run = functools.partial(on_device, mesh.shape["tm"], mesh.shape["chan"])
    return jax.shard_map(run, mesh=mesh, in_specs=placed, out_specs=P("tm"), check_vma=False)
```

time: 37.8 us -> 37.7 us (level)
  waiting for transfers between devices: 10.9 us -> 9.61 us
  Pallas kernels: 12.1 us -> 13.2 us
    ppermute x4, waiting for transfers between devices: 5.57 us -> 4.36 us  [shifted(): return lax.ppermute(value, axes, pairs)]
    pallas_call x2 -> x3, Pallas kernels: 12.1 us -> 13.2 us  [the longest x1 7.18 us: crossed(): pl.pallas_call(cross_body, out_shape=[sized(4, count // 4)] * 2, in_specs...]
  transfers between devices with their start and end apart: 6 -> 6, of which waited for: 5 -> 4; matrix products, arithmetic and copies ran while one was open for 0% -> 0% of each run, Pallas kernels for 3% -> 16%
where the time goes in v3:
time: 37.7 us; the launch traced here: 37.4 us
  Pallas kernels  13.2 us (35%)
  starting transfers between devices  12.1 us (32%)
  waiting for transfers between devices  9.61 us (25%)
  other arithmetic  1.48 us (4%)
  between operations  0.79 us (2%)
    ppermute x4, starting transfers between devices, shifted(): return lax.ppermute(value, axes, pairs)  8.97 us
    pallas_call x1, Pallas kernels, crossed(): pl.pallas_call(cross_body, out_shape=[sized(4, count // 4)] * 2, in_specs...  7.18 us
    ppermute x2, waiting for transfers between devices, swapped(): lax.ppermute(value, 'chan', [(c, chans - 1 - c) for c in range(chans)])  5.26 us
    ppermute x4, waiting for transfers between devices, shifted(): return lax.ppermute(value, axes, pairs)  4.36 us
    pallas_call x1, Pallas kernels, paired(): pl.pallas_call(pair_body, out_shape=sized(4, count // 4), in_specs=[SMEM]...  3.34 us
    ppermute x2, starting transfers between devices, swapped(): lax.ppermute(value, 'chan', [(c, chans - 1 - c) for c in range(chans)])  3.13 us
    pallas_call x1, Pallas kernels, prepare(): pl.pallas_call(own_body, out_shape=sized(count, channels * window, dtype=...  2.72 us
    concatenate x1, other arithmetic, profile(): jnp.concatenate([series, tail, spare], axis=1)  0.87 us
  transfers between devices with their start and end apart: 6, of which 4 were waited for; matrix products, arithmetic and copies ran while one was open for 0% of the time, Pallas kernels for 16%

profile of v3, /device:TPU:0, one launch (start us, length us, event | category | flops | bytes accessed | tf_op | source)
XLA Modules:
  0.0 37.4 jit_solution(5812278390255835306)
XLA Ops:
  0.0 0.1 pad.6.clone
  0.1 0.9 %maximum_maximum_fusion = f32[32,640]{1,0:T(8,128)S(1)} fusion(f32[32,127]{1,0:T(8,128)} %param.4, f32[32,512]{1,0:T(8,128)} %param.3, f32[640]{0:T(1024)S(1)} %pad.6.clone), kind=kLoop, calls=%fused_computation.3 | loop fusion | flops 40960 | bytes 166272 | tf_op jit(solution)/shard_map/concatenate | solution.py:282
  0.9 3.1 %collective-permute-start = (f32[32,640]{1,0:T(8,128)S(1)}, f32[32,640]{1,0:T(8,128)S(1)}, u32[]{:S(2)}, u32[]{:S(2)}) collective-permute-start(f32[32,640]{1,0:T(8,128)S(1)} %maximum_maximum_fusion), channel_id=1, source_target_pairs={{0,1},{1,0},{2,3},{3,2},{4,5},{5,4},{6,7},{7,6},{8,9},{9,8},{10,11... | collective-permute-start | bytes 245768 | tf_op jit(solution)/shard_map/ppermute | solution.py:276
  4.7 0.1 stack.35.info
  4.8 1.7 %collective-permute-done = f32[32,640]{1,0:T(8,128)S(1)} collective-permute-done((f32[32,640]{1,0:T(8,128)S(1)}, f32[32,640]{1,0:T(8,128)S(1)}, u32[]{:S(2)}, u32[]{:S(2)}) %collective-permute-start) | collective-permute-done | bytes 81952 | tf_op jit(solution)/shard_map/ppermute | solution.py:276
  6.5 1.3 %collective-permute-start.1 = (f32[64,128]{1,0:T(8,128)S(1)}, f32[64,128]{1,0:T(8,128)S(1)}, u32[]{:S(2)}, u32[]{:S(2)}) collective-permute-start(f32[64,128]{1,0:T(8,128)S(1)} %fusion), channel_id=1, source_target_pairs={{2,0},{3,1},{4,2},{5,3},{6,4},{7,5},{8,6},{9,7},{10,8},{11,9},{12,... | collective-permute-start | bytes 98312 | tf_op jit(solution)/shard_map/ppermute | solution.py:273
  7.8 1.3 %collective-permute-start.3 = (f32[64,128]{1,0:T(8,128)S(1)}, f32[64,128]{1,0:T(8,128)S(1)}, u32[]{:S(2)}, u32[]{:S(2)}) collective-permute-start(f32[64,128]{1,0:T(8,128)S(1)} %fusion), channel_id=1, source_target_pairs={{6,0},{5,1},{8,2},{7,3},{10,4},{9,5},{12,6},{11,7},{14,8},{13,9},{... | collective-permute-start | bytes 98312 | tf_op jit(solution)/shard_map/ppermute | solution.py:273
  9.1 1.3 %collective-permute-start.2 = (f32[64,512]{1,0:T(8,128)S(1)}, f32[64,512]{1,0:T(8,128)S(1)}, u32[]{:S(2)}, u32[]{:S(2)}) collective-permute-start(f32[64,512]{1,0:T(8,128)S(1)} %pad_maximum_fusion.near), channel_id=1, source_target_pairs={{4,0},{3,1},{6,2},{5,3},{8,4},{7,5},{10,6},{9,7},{12,8},{11,9},{14... | collective-permute-start | bytes 393224 | tf_op jit(solution)/shard_map/ppermute | solution.py:273
  10.4 0.0 collective-permute-done.1.head
  10.4 2.7 %shard_map.37.mine = bf16[512,8192]{1,0:T(8,128)(2,1)S(1)} custom-call(s32[6]{0:T(128)S(1)} %stack.35.info, f32[64,512]{1,0:T(8,128)S(1)} %pad_maximum_fusion.near, f32[64,128]{1,0:T(8,128)S(1)} %collective-permute-done.1.head, f32[64,128]{1,0:T(8,128)S(1)} %pad_maximum_fusion.1.tail), custom_call_target="tpu_custom_call" | custom-call | flops 419430400 | bytes 2097152 | tf_op jit(solution)/shard_map/pallas_call | solution.py:213
  13.1 0.8 %collective-permute-done.3.head = f32[64,128]{1,0:T(8,128)S(1)} collective-permute-done((f32[64,128]{1,0:T(8,128)S(1)}, f32[64,128]{1,0:T(8,128)S(1)}, u32[]{:S(2)}, u32[]{:S(2)}) %collective-permute-start.3) | collective-permute-done | bytes 32800 | tf_op jit(solution)/shard_map/ppermute | solution.py:273
  14.0 3.5 %collective-permute-done.2.other = f32[64,512]{1,0:T(8,128)S(1)} collective-permute-done((f32[64,512]{1,0:T(8,128)S(1)}, f32[64,512]{1,0:T(8,128)S(1)}, u32[]{:S(2)}, u32[]{:S(2)}) %collective-permute-start.2) | collective-permute-done | bytes 131104 | tf_op jit(solution)/shard_map/ppermute | solution.py:273
  17.5 7.2 %shard_map.38 = (f32[4,128]{1,0:T(4,128)S(1)}, f32[4,128]{1,0:T(4,128)S(1)}) custom-call(s32[6]{0:T(128)S(1)} %stack.35.info, bf16[512,8192]{1,0:T(8,128)(2,1)S(1)} %shard_map.37.mine, f32[64,512]{1,0:T(8,128)S(1)} %collective-permute-done.2.other, f32[64,128]{1,0:T(8,128)S(1)} %collective-permute-done.3.head, f32[64,128]{1,0:T(8,128)S(1)} %pad_maximum_fusion.1.tail), custom_call_target="tpu_custom_call" | custom-call | flops 4294967296 | bytes 2097152 | tf_op jit(solution)/shard_map/pallas_call | solution.py:226
  24.7 5.1 %collective-permute-start.4 = (f32[4,128]{1,0:T(4,128)S(1)}, f32[4,128]{1,0:T(4,128)S(1)}, u32[]{:S(2)}, u32[]{:S(2)}) collective-permute-start(f32[4,128]{1,0:T(4,128)S(1)} %get-tuple-element.8), channel_id=1, source_target_pairs={{1,3},{0,4},{3,5},{2,6},{5,7},{4,8},{7,9},{6,10},{9,11},{8,12},{11... | collective-permute-start | bytes 6152 | tf_op jit(solution)/shard_map/ppermute | solution.py:273
  29.8 3.3 %shard_map.39 = f32[4,128]{1,0:T(4,128)S(1)} custom-call(s32[6]{0:T(128)S(1)} %stack.35.info, bf16[512,8192]{1,0:T(8,128)(2,1)S(1)} %shard_map.37.mine, f32[4,128]{1,0:T(4,128)S(1)} %get-tuple-element.7.part), custom_call_target="tpu_custom_call" | custom-call | flops 2147483648 | bytes 2097152 | tf_op jit(solution)/shard_map/pallas_call | solution.py:242
  33.1 0.0 collective-permute-done.4
  33.2 0.1 collective-permute-start.5
  33.2 3.6 %collective-permute-done.5 = f32[4,128]{1,0:T(4,128)S(1)} collective-permute-done((f32[4,128]{1,0:T(4,128)S(1)}, f32[4,128]{1,0:T(4,128)S(1)}, u32[]{:S(2)}, u32[]{:S(2)}) %collective-permute-start.5) | collective-permute-done | bytes 2080 | tf_op jit(solution)/shard_map/ppermute | solution.py:276
  36.8 0.6 %minimum_bitcast_fusion = f32[512]{0:T(512)} fusion(f32[4,128]{1,0:T(4,128)S(1)} %select_minimum_fusion, f32[4,128]{1,0:T(4,128)S(1)} %collective-permute-done.5), kind=kLoop, calls=%fused_computation.6 | loop fusion | flops 512 | bytes 6144 | tf_op jit(solution)/shard_map/reshape | solution.py:294
  (8 shorter events, 0.0 us)
Async XLA Ops:
  0.9 5.5 %collective-permute-start = (f32[32,640]{1,0:T(8,128)S(1)}, f32[32,640]{1,0:T(8,128)S(1)}, u32[]{:S(2)}, u32[]{:S(2)}) collective-permute-start(f32[32,640]{1,0:T(8,128)S(1)} %maximum_maximum_fusion), channel_id=1, source_target_pairs={{0,1},{1,0},{2,3},{3,2},{4,5},{5,4},{6,7},{7,6},{8,9},{9,8},{10,11... | collective-permute-start | bytes 245768 | tf_op jit(solution)/shard_map/ppermute | solution.py:276
  6.5 3.9 %collective-permute-start.1 = (f32[64,128]{1,0:T(8,128)S(1)}, f32[64,128]{1,0:T(8,128)S(1)}, u32[]{:S(2)}, u32[]{:S(2)}) collective-permute-start(f32[64,128]{1,0:T(8,128)S(1)} %fusion), channel_id=1, source_target_pairs={{2,0},{3,1},{4,2},{5,3},{6,4},{7,5},{8,6},{9,7},{10,8},{11,9},{12,... | collective-permute-start | bytes 98312 | tf_op jit(solution)/shard_map/ppermute | solution.py:273
  7.8 6.2 %collective-permute-start.3 = (f32[64,128]{1,0:T(8,128)S(1)}, f32[64,128]{1,0:T(8,128)S(1)}, u32[]{:S(2)}, u32[]{:S(2)}) collective-permute-start(f32[64,128]{1,0:T(8,128)S(1)} %fusion), channel_id=1, source_target_pairs={{6,0},{5,1},{8,2},{7,3},{10,4},{9,5},{12,6},{11,7},{14,8},{13,9},{... | collective-permute-start | bytes 98312 | tf_op jit(solution)/shard_map/ppermute | solution.py:273
  9.1 8.4 %collective-permute-start.2 = (f32[64,512]{1,0:T(8,128)S(1)}, f32[64,512]{1,0:T(8,128)S(1)}, u32[]{:S(2)}, u32[]{:S(2)}) collective-permute-start(f32[64,512]{1,0:T(8,128)S(1)} %pad_maximum_fusion.near), channel_id=1, source_target_pairs={{4,0},{3,1},{6,2},{5,3},{8,4},{7,5},{10,6},{9,7},{12,8},{11,9},{14... | collective-permute-start | bytes 393224 | tf_op jit(solution)/shard_map/ppermute | solution.py:273
  24.7 8.4 %collective-permute-start.4 = (f32[4,128]{1,0:T(4,128)S(1)}, f32[4,128]{1,0:T(4,128)S(1)}, u32[]{:S(2)}, u32[]{:S(2)}) collective-permute-start(f32[4,128]{1,0:T(4,128)S(1)} %get-tuple-element.8), channel_id=1, source_target_pairs={{1,3},{0,4},{3,5},{2,6},{5,7},{4,8},{7,9},{6,10},{9,11},{8,12},{11... | collective-permute-start | bytes 6152 | tf_op jit(solution)/shard_map/ppermute | solution.py:273
  33.2 3.7 %collective-permute-start.5 = (f32[4,128]{1,0:T(4,128)S(1)}, f32[4,128]{1,0:T(4,128)S(1)}, u32[]{:S(2)}, u32[]{:S(2)}) collective-permute-start(f32[4,128]{1,0:T(4,128)S(1)} %select_minimum_fusion), channel_id=1, source_target_pairs={{0,1},{1,0},{2,3},{3,2},{4,5},{5,4},{6,7},{7,6},{8,9},{9,8},{10,11... | collective-permute-start | bytes 6152 | tf_op jit(solution)/shard_map/ppermute | solution.py:276

commit v4 on v3

--- a/solution.py
+++ b/solution.py
@@ -116,13 +116,27 @@
     lax.fori_loop(0, zed_out.shape[1] // (WIDTH * LANES), build, 0)
 
 
+def staged(mine, stage, base, chan):
+    quarter = mine.shape[0] // 4
+    for place in range(2):
+        start = pl.multiple_of((2 * place + chan) * quarter, quarter)
+        stage[place * quarter : (place + 1) * quarter, :] = mine[
+            pl.ds(start, quarter), pl.ds(base, WIDTH * LANES)
+        ]
+
+
 def cross_body(
-    info, mine, other, head, tail, away_out, part_out,
+    info, mine, other, head, tail, away_out, part_out, pair_out,
     samples, means, scales, sums_a, sums_b, moments_a, moments_b, zed_a, zed_b, cross,
+    stage_a, stage_b,
 ):
     count = means.shape[0]
     quarter = count // 4
     limit, shift, valid = info[0], info[2], info[3]
+    for block, stage in enumerate((stage_a, stage_b)):
+        staged(mine, stage, block_of(block), info[1])
+        value = contract(mine[:, pl.ds(block_of(block), WIDTH * LANES)], stage[...])
+        pair_out[...] = pair_out[...] + value if block else value
     last = jnp.where(info[5] > 0, tail[...], head[...])
     transposed(jnp.concatenate([other[...], last], axis=1), samples)
     statistics(
@@ -152,7 +166,7 @@
         part_out[index : index + 1, :] = columns[:, rows]
 
 
-def pair_body(info, mine, part, own_out, stage_a, stage_b, pair):
+def pair_body(info, mine, part, partial, own_out, stage_a, stage_b, pair):
     count = mine.shape[0]
     quarter = count // 4
     limit, chan = info[0], info[1]
@@ -161,19 +175,12 @@
         pl.multiple_of(chan * quarter, quarter),
         pl.multiple_of(2 * quarter + chan * quarter, quarter),
     ]
-    pair[...] = jnp.zeros_like(pair)
-
-    def step(index, carry):
-        for slot in range(2):
-            lanes = pl.ds(block_of(2 * index + slot), WIDTH * LANES)
-            for place, start in enumerate(starts):
-                stages[slot][place * quarter : (place + 1) * quarter, :] = mine[
-                    pl.ds(start, quarter), lanes
-                ]
-            pair[...] += contract(mine[:, lanes], stages[slot][...])
-        return carry
-
-    lax.fori_loop(0, mine.shape[1] // (2 * WIDTH * LANES), step, 0)
+    blocks = mine.shape[1] // (WIDTH * LANES)
+    for slot in range(2):
+        base = block_of(blocks - 2 + slot)
+        staged(mine, stages[slot], base, chan)
+        value = contract(mine[:, pl.ds(base, WIDTH * LANES)], stages[slot][...])
+        pair[...] = (pair if slot else partial)[...] + value
     near = []
     for index, start in enumerate(starts):
         value = pair[:, index * quarter : (index + 1) * quarter]
@@ -225,31 +232,32 @@
     window = head.shape[1]
     return pl.pallas_call(
         cross_body,
-        out_shape=[sized(4, count // 4)] * 2,
+        out_shape=[sized(4, count // 4)] * 2 + [sized(count, count // 2)],
         in_specs=[SMEM] + [VMEM] * 4,
-        out_specs=[VMEM] * 2,
+        out_specs=[VMEM] * 3,
         scratch_shapes=[
             *working(count, count + window),
             *[pltpu.VMEM((count, WIDTH * LANES), jnp.bfloat16)] * 2,
             pltpu.VMEM((count, count), jnp.float32),
+            *[pltpu.VMEM((count // 2, WIDTH * LANES), jnp.bfloat16)] * 2,
         ],
         **settings(2 * count * count * channels * window),
     )(info, mine, other, head, tail)
 
 
-def paired(info, mine, part):
+def paired(info, mine, part, partial):
     count, depth = mine.shape
     return pl.pallas_call(
         pair_body,
         out_shape=sized(4, count // 4),
-        in_specs=[SMEM] + [VMEM] * 2,
+        in_specs=[SMEM] + [VMEM] * 3,
         out_specs=VMEM,
         scratch_shapes=[
             *[pltpu.VMEM((count // 2, WIDTH * LANES), jnp.bfloat16)] * 2,
             pltpu.VMEM((count, count // 2), jnp.float32),
         ],
         **settings(count * count * depth),
-    )(info, mine, part)
+    )(info, mine, part, partial)
 
 
 def on_device(blocks, chans, series, tail, excl):
@@ -279,17 +287,21 @@
     flags = [block + shift < blocks, block == blocks - 1, block + shift == blocks - 1]
     info = jnp.stack([excl[0], chan, shift] + [flag.astype(jnp.int32) for flag in flags])
     spare = jnp.zeros((series.shape[0], 1), series.dtype)
+    partner = swapped(series)
+    ends = [(b, c) for b, c in places if b >= blocks - 1 - chans]
+    pairs = [(b * chans + c, b * chans + chans - 1 - c) for b, c in ends]
+    partner_tail = lax.ppermute(tail, axes, pairs)
     padded = lax.optimization_barrier(jnp.concatenate([series, tail, spare], axis=1))
-    partner = swapped(padded)
-    near = jnp.concatenate([padded[:, :count], partner[:, :count]], axis=0)
-    ending = jnp.concatenate([padded[:, count:], partner[:, count:]], axis=0)
+    near = jnp.concatenate([padded[:, :count], partner], axis=0)
+    partner_tail = jnp.concatenate([partner_tail, spare], axis=1)
+    ending = jnp.concatenate([padded[:, count:], partner_tail], axis=0)
     other = shifted(near, lambda c: chans - c)
     head = shifted(near[:, :window], lambda c: 1)
     other_head = shifted(near[:, :window], lambda c: chans + 1 - c)
     mine = prepare(info, near, head, ending)
-    away, part = crossed(info, mine, other, other_head, ending)
+    away, part, partial = crossed(info, mine, other, other_head, ending)
     home = shifted(away, lambda c: c - chans)
-    best = paired(info, mine, part)
+    best = paired(info, mine, part, partial)
     best = jnp.minimum(best, jnp.where(block - shift >= 0, home, CEILING))
     return jnp.minimum(best, swapped(best)).reshape(count)
 

time: 37.7 us -> 36.1 us (0.958)
  the two profiles are of different devices: /device:TPU:0 before, /device:TPU:24 now
where the time goes in v4:
time: 36.1 us; the launch traced here: 35.8 us
  Pallas kernels  12.7 us (35%)
  starting transfers between devices  11.5 us (32%)
  waiting for transfers between devices  9.19 us (25%)
  other arithmetic  1.47 us (4%)
  between operations  0.79 us (2%)
    ppermute x4, starting transfers between devices, shifted(): return lax.ppermute(value, axes, pairs)  9.12 us
    pallas_call x1, Pallas kernels, crossed(): pl.pallas_call(cross_body, out_shape=[sized(4, count // 4)] * 2 + [sized(...  8.06 us
    ppermute x2, waiting for transfers between devices, swapped(): lax.ppermute(value, 'chan', [(c, chans - 1 - c) for c in range(chans)])  4.85 us
    ppermute x4, waiting for transfers between devices, shifted(): return lax.ppermute(value, axes, pairs)  4.33 us
    pallas_call x1, Pallas kernels, prepare(): pl.pallas_call(own_body, out_shape=sized(count, channels * window, dtype=...  2.72 us
    pallas_call x1, Pallas kernels, paired(): pl.pallas_call(pair_body, out_shape=sized(4, count // 4), in_specs=[SMEM]...  1.92 us
    ppermute x2, starting transfers between devices, swapped(): lax.ppermute(value, 'chan', [(c, chans - 1 - c) for c in range(chans)])  1.72 us
    concatenate x1, other arithmetic, profile(): jnp.concatenate([series, tail, spare], axis=1)  0.87 us
  transfers between devices with their start and end apart: 7, of which 4 were waited for; matrix products, arithmetic and copies ran while one was open for 3% of the time, Pallas kernels for 13%

profile of v4, /device:TPU:24, one launch (start us, length us, event | category | flops | bytes accessed | tf_op | source)
XLA Modules:
  0.0 35.8 jit_solution(1978034576991236298)
XLA Ops:
  0.0 0.7 %collective-permute-start.2 = (f32[32,127]{1,0:T(8,128)}, f32[32,127]{1,0:T(8,128)S(1)}, u32[]{:S(2)}, u32[]{:S(2)}) collective-permute-start(f32[32,127]{1,0:T(8,128)} %param.4), channel_id=1, source_target_pairs={{26,27},{27,26},{28,29},{29,28},{30,31},{31,30}} | collective-permute-start | bytes 48776 | tf_op jit(solution)/shard_map/ppermute | solution.py:293
  0.7 1.6 %collective-permute-start = (f32[32,512]{1,0:T(8,128)}, f32[32,512]{1,0:T(8,128)S(1)}, u32[]{:S(2)}, u32[]{:S(2)}) collective-permute-start(f32[32,512]{1,0:T(8,128)} %param.3), channel_id=1, source_target_pairs={{0,1},{1,0},{2,3},{3,2},{4,5},{5,4},{6,7},{7,6},{8,9},{9,8},{10,11... | collective-permute-start | bytes 196616 | tf_op jit(solution)/shard_map/ppermute | solution.py:284
  2.2 0.1 pad.7.clone
  2.3 0.9 %maximum_maximum_fusion = f32[32,640]{1,0:T(8,128)S(1)} fusion(f32[32,127]{1,0:T(8,128)} %param.4, f32[32,512]{1,0:T(8,128)} %param.3, f32[640]{0:T(1024)S(1)} %pad.7.clone), kind=kLoop, calls=%fused_computation.3 | loop fusion | flops 40960 | bytes 166272 | tf_op jit(solution)/shard_map/concatenate | solution.py:294
  3.9 0.1 stack.35.info
  4.0 1.4 %collective-permute-done = f32[32,512]{1,0:T(8,128)S(1)} collective-permute-done((f32[32,512]{1,0:T(8,128)}, f32[32,512]{1,0:T(8,128)S(1)}, u32[]{:S(2)}, u32[]{:S(2)}) %collective-permute-start) | collective-permute-done | bytes 65568 | tf_op jit(solution)/shard_map/ppermute | solution.py:284
  5.4 1.9 %collective-permute-start.1 = (f32[64,128]{1,0:T(8,128)S(1)}, f32[64,128]{1,0:T(8,128)S(1)}, u32[]{:S(2)}, u32[]{:S(2)}) collective-permute-start(f32[64,128]{1,0:T(8,128)S(1)} %fusion), channel_id=1, source_target_pairs={{2,0},{3,1},{4,2},{5,3},{6,4},{7,5},{8,6},{9,7},{10,8},{11,9},{12,... | collective-permute-start | bytes 98312 | tf_op jit(solution)/shard_map/ppermute | solution.py:281
  7.3 3.1 %collective-permute-start.3 = (f32[64,512]{1,0:T(8,128)S(1)}, f32[64,512]{1,0:T(8,128)S(1)}, u32[]{:S(2)}, u32[]{:S(2)}) collective-permute-start(f32[64,512]{1,0:T(8,128)S(1)} %pad_maximum_fusion.near), channel_id=1, source_target_pairs={{4,0},{3,1},{6,2},{5,3},{8,4},{7,5},{10,6},{9,7},{12,8},{11,9},{14... | collective-permute-start | bytes 393224 | tf_op jit(solution)/shard_map/ppermute | solution.py:281
  10.4 0.0 collective-permute-done.2
  10.5 2.2 %collective-permute-start.4 = (f32[64,128]{1,0:T(8,128)S(1)}, f32[64,128]{1,0:T(8,128)S(1)}, u32[]{:S(2)}, u32[]{:S(2)}) collective-permute-start(f32[64,128]{1,0:T(8,128)S(1)} %fusion), channel_id=1, source_target_pairs={{6,0},{5,1},{8,2},{7,3},{10,4},{9,5},{12,6},{11,7},{14,8},{13,9},{... | collective-permute-start | bytes 98312 | tf_op jit(solution)/shard_map/ppermute | solution.py:281
  12.6 0.0 collective-permute-done.1.head
  12.7 2.7 %shard_map.37.mine = bf16[512,8192]{1,0:T(8,128)(2,1)S(1)} custom-call(s32[6]{0:T(128)S(1)} %stack.35.info, f32[64,512]{1,0:T(8,128)S(1)} %pad_maximum_fusion.near, f32[64,128]{1,0:T(8,128)S(1)} %collective-permute-done.1.head, f32[64,128]{1,0:T(8,128)S(1)} %select_maximum_fusion.tail), custom_call_target="tpu_custom_call" | custom-call | flops 419430400 | bytes 2097152 | tf_op jit(solution)/shard_map/pallas_call | solution.py:220
  15.4 1.8 %collective-permute-done.4.head = f32[64,128]{1,0:T(8,128)S(1)} collective-permute-done((f32[64,128]{1,0:T(8,128)S(1)}, f32[64,128]{1,0:T(8,128)S(1)}, u32[]{:S(2)}, u32[]{:S(2)}) %collective-permute-start.4) | collective-permute-done | bytes 32800 | tf_op jit(solution)/shard_map/ppermute | solution.py:281
  17.2 0.0 collective-permute-done.3.other
  17.2 8.1 %shard_map.38 = (f32[4,128]{1,0:T(4,128)S(1)}, f32[4,128]{1,0:T(4,128)S(1)}, f32[512,256]{1,0:T(8,128)S(1)}) custom-call(s32[6]{0:T(128)S(1)} %stack.35.info, bf16[512,8192]{1,0:T(8,128)(2,1)S(1)} %shard_map.37.mine, f32[64,512]{1,0:T(8,128)S(1)} %collective-permute-done.3.other, f32[64,128]{1,0:T(8,128)S(1)} %collective-permute-done.4.head, ...), custom_call_target="tpu_custom_call" | custom-call | flops 4294967296 | bytes 2097152 | tf_op jit(solution)/shard_map/pallas_call | solution.py:233
  25.3 1.9 %collective-permute-start.5 = (f32[4,128]{1,0:T(4,128)S(1)}, f32[4,128]{1,0:T(4,128)S(1)}, u32[]{:S(2)}, u32[]{:S(2)}) collective-permute-start(f32[4,128]{1,0:T(4,128)S(1)} %get-tuple-element.10), channel_id=1, source_target_pairs={{1,3},{0,4},{3,5},{2,6},{5,7},{4,8},{7,9},{6,10},{9,11},{8,12},{11... | collective-permute-start | bytes 6152 | tf_op jit(solution)/shard_map/ppermute | solution.py:281
  27.2 1.9 %shard_map.39 = f32[4,128]{1,0:T(4,128)S(1)} custom-call(s32[6]{0:T(128)S(1)} %stack.35.info, bf16[512,8192]{1,0:T(8,128)(2,1)S(1)} %shard_map.37.mine, f32[4,128]{1,0:T(4,128)S(1)} %get-tuple-element.8.part, f32[512,256]{1,0:T(8,128)S(1)} %get-tuple-element.9.partial), custom_call_target="tpu_custom_call" | custom-call | flops 2147483648 | bytes 2097152 | tf_op jit(solution)/shard_map/pallas_call | solution.py:250
  29.1 2.5 %collective-permute-done.5 = f32[4,128]{1,0:T(4,128)S(1)} collective-permute-done((f32[4,128]{1,0:T(4,128)S(1)}, f32[4,128]{1,0:T(4,128)S(1)}, u32[]{:S(2)}, u32[]{:S(2)}) %collective-permute-start.5) | collective-permute-done | bytes 2080 | tf_op jit(solution)/shard_map/ppermute | solution.py:281
  31.6 0.1 collective-permute-start.6
  31.8 3.5 %collective-permute-done.6 = f32[4,128]{1,0:T(4,128)S(1)} collective-permute-done((f32[4,128]{1,0:T(4,128)S(1)}, f32[4,128]{1,0:T(4,128)S(1)}, u32[]{:S(2)}, u32[]{:S(2)}) %collective-permute-start.6) | collective-permute-done | bytes 2080 | tf_op jit(solution)/shard_map/ppermute | solution.py:284
  35.2 0.6 %minimum_bitcast_fusion = f32[512]{0:T(512)} fusion(f32[4,128]{1,0:T(4,128)S(1)} %select_minimum_fusion, f32[4,128]{1,0:T(4,128)S(1)} %collective-permute-done.6), kind=kLoop, calls=%fused_computation.7 | loop fusion | flops 512 | bytes 6144 | tf_op jit(solution)/shard_map/reshape | solution.py:306
  (6 shorter events, 0.0 us)
Async XLA Ops:
  0.0 10.4 %collective-permute-start.2 = (f32[32,127]{1,0:T(8,128)}, f32[32,127]{1,0:T(8,128)S(1)}, u32[]{:S(2)}, u32[]{:S(2)}) collective-permute-start(f32[32,127]{1,0:T(8,128)} %param.4), channel_id=1, source_target_pairs={{26,27},{27,26},{28,29},{29,28},{30,31},{31,30}} | collective-permute-start | bytes 48776 | tf_op jit(solution)/shard_map/ppermute | solution.py:293
  0.7 4.7 %collective-permute-start = (f32[32,512]{1,0:T(8,128)}, f32[32,512]{1,0:T(8,128)S(1)}, u32[]{:S(2)}, u32[]{:S(2)}) collective-permute-start(f32[32,512]{1,0:T(8,128)} %param.3), channel_id=1, source_target_pairs={{0,1},{1,0},{2,3},{3,2},{4,5},{5,4},{6,7},{7,6},{8,9},{9,8},{10,11... | collective-permute-start | bytes 196616 | tf_op jit(solution)/shard_map/ppermute | solution.py:284
  5.4 7.3 %collective-permute-start.1 = (f32[64,128]{1,0:T(8,128)S(1)}, f32[64,128]{1,0:T(8,128)S(1)}, u32[]{:S(2)}, u32[]{:S(2)}) collective-permute-start(f32[64,128]{1,0:T(8,128)S(1)} %fusion), channel_id=1, source_target_pairs={{2,0},{3,1},{4,2},{5,3},{6,4},{7,5},{8,6},{9,7},{10,8},{11,9},{12,... | collective-permute-start | bytes 98312 | tf_op jit(solution)/shard_map/ppermute | solution.py:281
  7.3 9.9 %collective-permute-start.3 = (f32[64,512]{1,0:T(8,128)S(1)}, f32[64,512]{1,0:T(8,128)S(1)}, u32[]{:S(2)}, u32[]{:S(2)}) collective-permute-start(f32[64,512]{1,0:T(8,128)S(1)} %pad_maximum_fusion.near), channel_id=1, source_target_pairs={{4,0},{3,1},{6,2},{5,3},{8,4},{7,5},{10,6},{9,7},{12,8},{11,9},{14... | collective-permute-start | bytes 393224 | tf_op jit(solution)/shard_map/ppermute | solution.py:281
  10.5 6.7 %collective-permute-start.4 = (f32[64,128]{1,0:T(8,128)S(1)}, f32[64,128]{1,0:T(8,128)S(1)}, u32[]{:S(2)}, u32[]{:S(2)}) collective-permute-start(f32[64,128]{1,0:T(8,128)S(1)} %fusion), channel_id=1, source_target_pairs={{6,0},{5,1},{8,2},{7,3},{10,4},{9,5},{12,6},{11,7},{14,8},{13,9},{... | collective-permute-start | bytes 98312 | tf_op jit(solution)/shard_map/ppermute | solution.py:281
  25.3 6.4 %collective-permute-start.5 = (f32[4,128]{1,0:T(4,128)S(1)}, f32[4,128]{1,0:T(4,128)S(1)}, u32[]{:S(2)}, u32[]{:S(2)}) collective-permute-start(f32[4,128]{1,0:T(4,128)S(1)} %get-tuple-element.10), channel_id=1, source_target_pairs={{1,3},{0,4},{3,5},{2,6},{5,7},{4,8},{7,9},{6,10},{9,11},{8,12},{11... | collective-permute-start | bytes 6152 | tf_op jit(solution)/shard_map/ppermute | solution.py:281
  31.6 3.6 %collective-permute-start.6 = (f32[4,128]{1,0:T(4,128)S(1)}, f32[4,128]{1,0:T(4,128)S(1)}, u32[]{:S(2)}, u32[]{:S(2)}) collective-permute-start(f32[4,128]{1,0:T(4,128)S(1)} %select_minimum_fusion), channel_id=1, source_target_pairs={{0,1},{1,0},{2,3},{3,2},{4,5},{5,4},{6,7},{7,6},{8,9},{9,8},{10,11... | collective-permute-start | bytes 6152 | tf_op jit(solution)/shard_map/ppermute | solution.py:284
